TPU v7x, 128 devices: a whole 4x4x4 slice. The times are simulated.
128 devices in a mesh: ctx: 16 (over y, x), mem: 4 (over z), half: 2 (over core).
Axes of the slice: x: 4, y: 4, z: 4, core: 2. Of those that a mesh axis runs over, the one named last changes fastest.
Arguments:
- tokens: bfloat16 [32768, 2048], P(('ctx', 'mem')), may hold values from -6 to 6
- routes: int32 [32768, 1], P(('ctx', 'mem')), may hold values from 0 to 15; in each aligned block of 512 rows (0 to 511, 512 to 1023, ...) at most 64 rows name the same one
- w_query: bfloat16 [2048, 1024], P(None, 'half'), may hold values from -0.125 to 0.125
- w_key: bfloat16 [16, 2048, 1024], P('mem', None, 'half'), may hold values from -0.125 to 0.125
- w_value: bfloat16 [16, 2048, 1024], P('mem', None, 'half'), may hold values from -0.125 to 0.125
- w_beta: bfloat16 [16, 2048, 8], P('mem', None, 'half'), may hold values from -0.125 to 0.125
- w_decay: bfloat16 [16, 2048, 8], P('mem', None, 'half'), may hold values from -0.125 to 0.125
- decay_rate: float32 [16, 8], P('mem', 'half'), may hold values from 0.002 to 0.2
- norm_gain: float32 [1024], P('half'), may hold values from 0.1 to 1.9
- w_out: bfloat16 [1024, 2048], P('half'), may hold values from -0.1875 to 0.1875
Outputs:
- mixed: bfloat16 [32768, 2048], P(('ctx', 'mem', 'half'))
Inputs may be any that keep to these rules, and one draw needn't show every extreme that they name: `routes`: each token names one memory. Within each aligned block of 512 rows no memory is named by more than 64 rows, and in some blocks one memory is named by exactly 64 rows.
All inputs are finite; a program needn't handle non-finite values.
Results may differ from a plain program's by a relative error of at most 0.0049.
Values may be sent and summed in bfloat16 or wider, within the bound.
A program may use at most 192 MiB of HBM per device.

v0:
```python
import jax
import jax.numpy as jnp
from jax import lax
from jax.sharding import PartitionSpec as P

BLOCK = 64


def shifted(shard, axis, by):
    devices = lax.axis_size(axis)
    pairs = [(i, i + by) for i in range(devices) if 0 <= i + by < devices]
    return lax.ppermute(shard, axis, pairs)


def normalize_heads(vectors):
    return vectors / jnp.sqrt(jnp.sum(vectors * vectors, axis=-1, keepdims=True) + 1e-06)


def per_device(
    tokens, routes, w_query, w_key, w_value, w_beta, w_decay, decay_rate, norm_gain, w_out
):
    precise_result = lax.Precision.HIGHEST
    tok_rows, width = tokens.shape
    mem_local = w_key.shape[0]
    owners = lax.axis_size("mem")
    memories = mem_local * owners
    capacity = tok_rows // 8
    heads_here = decay_rate.shape[1]
    key_size = w_key.shape[2] // heads_here
    value_size = w_value.shape[2] // heads_here
    route = routes[:, 0]
    member = (route[:, None] == jnp.arange(memories, dtype=jnp.int32)[None, :]).astype(jnp.int32)
    places = jnp.sum(jnp.cumsum(member, axis=0) * member, axis=1) - 1
    slots = route * capacity + places
    outgoing = jnp.zeros((memories * capacity, width), jnp.bfloat16).at[slots].set(tokens)
    present = (
        jnp.zeros((memories * capacity,), jnp.bfloat16)
        .at[slots]
        .set(jnp.ones((tok_rows,), jnp.bfloat16))
    )
    outgoing = outgoing.reshape(owners, mem_local, capacity, width)
    present = present.reshape(owners, mem_local, capacity)
    arrived, live = (
        lax.all_to_all(outgoing, "mem", split_axis=0, concat_axis=0, tiled=True),
        lax.all_to_all(present, "mem", split_axis=0, concat_axis=0, tiled=True),
    )
    span = owners * capacity
    batch = mem_local * heads_here
    count = span // BLOCK
    query = jnp.einsum(
        "smcd,dhk->mhsck",
        arrived,
        w_query.reshape(width, heads_here, key_size),
        preferred_element_type=jnp.float32,
    )
    keys = jnp.einsum(
        "smcd,mdhk->mhsck",
        arrived,
        w_key.reshape(mem_local, width, heads_here, key_size),
        preferred_element_type=jnp.float32,
    )
    values = jnp.einsum(
        "smcd,mdhk->mhsck",
        arrived,
        w_value.reshape(mem_local, width, heads_here, value_size),
        preferred_element_type=jnp.float32,
    )
    beta_logit = jnp.einsum("smcd,mdh->mhsc", arrived, w_beta, preferred_element_type=jnp.float32)
    decay_logit = jnp.einsum("smcd,mdh->mhsc", arrived, w_decay, preferred_element_type=jnp.float32)
    live_slots = jnp.transpose(live, (1, 0, 2)).reshape(mem_local, 1, span).astype(jnp.float32)
    strength = jax.nn.sigmoid(beta_logit.reshape(mem_local, heads_here, span)) * live_slots
    forget = (
        -decay_rate[:, :, None]
        * jax.nn.softplus(decay_logit.reshape(mem_local, heads_here, span))
        * live_slots
    )
    query = normalize_heads(query.reshape(batch, count, BLOCK, key_size))
    keys = normalize_heads(keys.reshape(batch, count, BLOCK, key_size))
    values = values.reshape(batch, count, BLOCK, value_size)
    strength = strength.reshape(batch, count, BLOCK)
    forget = forget.reshape(batch, count, BLOCK)
    running = jnp.cumsum(forget, axis=-1)
    row_index = jnp.arange(BLOCK, dtype=jnp.int32)
    inclusive = (row_index[:, None] >= row_index[None, :]).astype(jnp.float32)
    strict = (row_index[:, None] > row_index[None, :]).astype(jnp.float32)
    spread = running[..., :, None] - running[..., None, :]
    decay_pair = jnp.exp(jnp.where(inclusive > 0, spread, 0.0)) * inclusive
    intersection = jnp.einsum("bnik,bnjk->bnij", keys, keys, precision=precise_result)
    coupling = intersection * decay_pair * strength[..., :, None] * strict
    identity_block = jnp.eye(BLOCK, dtype=jnp.float32)
    inverse = identity_block - coupling
    power = coupling
    covered = 2
    while covered < BLOCK:
        power = jnp.einsum("bnij,bnjk->bnik", power, power, precision=precise_result)
        inverse = jnp.einsum(
            "bnij,bnjk->bnik", inverse, identity_block + power, precision=precise_result
        )
        covered = covered * 2
    targets = jnp.concatenate(
        [(strength * jnp.exp(running))[..., None] * keys, strength[..., None] * values], axis=-1
    )
    solved = jnp.einsum("bnij,bnjc->bnic", inverse, targets, precision=precise_result)
    w_part = solved[..., :key_size]
    u_part = solved[..., key_size:]
    tail = jnp.exp(running[..., -1:] - running)
    key_tail = keys * tail[..., None]
    identity_key = jnp.eye(key_size, dtype=jnp.float32)
    transit = jnp.exp(running[..., -1])[..., None, None] * identity_key - jnp.einsum(
        "bnik,bnil->bnkl", key_tail, w_part, precision=precise_result
    )
    written = jnp.einsum("bnik,bniv->bnkv", key_tail, u_part, precision=precise_result)
    scores = jnp.einsum("bnik,bnjk->bnij", query, keys, precision=precise_result) * decay_pair
    local_out = jnp.einsum("bnij,bnjv->bniv", scores, u_part, precision=precise_result)
    reach = query * jnp.exp(running)[..., None] - jnp.einsum(
        "bnij,bnjk->bnik", scores, w_part, precision=precise_result
    )

    def through_blocks(carry, item):
        product, accrued = carry
        transit_now, written_now, out_now, reach_now = item
        base = out_now + jnp.einsum("bik,bkv->biv", reach_now, accrued, precision=precise_result)
        carried = jnp.einsum("bik,bkl->bil", reach_now, product, precision=precise_result)
        product = jnp.einsum("bkl,blm->bkm", transit_now, product, precision=precise_result)
        accrued = (
            jnp.einsum("bkl,blv->bkv", transit_now, accrued, precision=precise_result) + written_now
        )
        return ((product, accrued), (base, carried))

    start_map = jnp.broadcast_to(identity_key, (batch, key_size, key_size))
    start_state = jnp.zeros((batch, key_size, value_size), jnp.float32)
    block_items = (
        jnp.swapaxes(transit, 0, 1),
        jnp.swapaxes(written, 0, 1),
        jnp.swapaxes(local_out, 0, 1),
        jnp.swapaxes(reach, 0, 1),
    )
    (whole_map, whole_state), (base_out, carried_map) = lax.scan(
        through_blocks, (start_map, start_state), block_items
    )

    def forward_state_update(turn, carry):
        incoming, leaving = carry
        incoming = shifted(leaving, "ctx", 1)
        leaving = (
            jnp.einsum("bkl,blv->bkv", whole_map, incoming, precision=precise_result) + whole_state
        )
        return (incoming, leaving)

    entering, _ = lax.fori_loop(
        0, lax.axis_size("ctx") - 1, forward_state_update, (start_state, whole_state)
    )
    heads_out = base_out + jnp.einsum(
        "nbik,bkv->nbiv", carried_map, entering, precision=precise_result
    )
    scale = 1.0 / jnp.sqrt(jnp.mean(heads_out * heads_out, axis=-1, keepdims=True) + 1e-05)
    gain_rows = jnp.tile(norm_gain.reshape(heads_here, value_size), (mem_local, 1))
    normalized_rows = heads_out * scale * gain_rows[None, :, None, :]
    normalized_rows = normalized_rows.reshape(count, mem_local, heads_here, BLOCK, value_size)
    normalized_rows = jnp.transpose(normalized_rows, (1, 0, 3, 2, 4)).reshape(
        mem_local, owners, capacity, heads_here * value_size
    )
    reply = jnp.transpose(normalized_rows, (1, 0, 2, 3)).astype(jnp.bfloat16)
    returned = lax.all_to_all(reply, "mem", split_axis=0, concat_axis=0, tiled=True)
    returned = returned.reshape(memories * capacity, heads_here * value_size)
    picked = returned[slots]
    mixed = lax.psum_scatter(
        jnp.dot(picked, w_out, preferred_element_type=jnp.float32),
        "half",
        scatter_dimension=0,
        tiled=True,
    )
    return mixed.astype(jnp.bfloat16)


def solution(mesh):
    in_specs = (
        P(("ctx", "mem"), None),
        P(("ctx", "mem"), None),
        P(None, "half"),
        P("mem", None, "half"),
        P("mem", None, "half"),
        P("mem", None, "half"),
        P("mem", None, "half"),
        P("mem", "half"),
        P("half"),
        P("half", None),
    )
    out_specs = P(("ctx", "mem", "half"), None)
    return jax.shard_map(
        per_device, mesh=mesh, in_specs=in_specs, out_specs=out_specs, check_vma=False
    )
```

profile of v0, /device:TPU:25, one launch (start us, length us, event | category | flops | bytes accessed | tf_op | source)
XLA Modules:
  0.0 674.5 jit_solution(17416910878021449122)
XLA Ops:
  14.8 5.0 all-to-all-start.1
  19.8 7.2 %scatter_custom_fusion = bf16[1024,2048]{1,0:T(8,128)(2,1)} fusion(s32[512]{0:T(512)S(1)} %bitcast.203, bf16[512,2048]{1,0:T(8,128)(2,1)} %param.14, bf16[]{:T(256)} %constant.24.clone.1), kind=kCustom, calls=%fused_computation.74 | custom fusion | bytes 4194816 | tf_op jit(solution)/shard_map/scatter | solution.py:35
  27.0 5.2 all-to-all-start
  32.4 12.5 %reshape.211 = bf16[4,2048,4,128]{3,2,1,0:T(4,128)(2,1)} reshape(bf16[4,2048,512]{2,1,0:T(8,128)(2,1)} %param.17) | data formatting | bytes 16777216 | tf_op jit(solution)/shard_map/reshape | solution.py:59
  44.9 12.5 %reshape.213 = bf16[4,2048,4,128]{3,2,1,0:T(4,128)(2,1)} reshape(bf16[4,2048,512]{2,1,0:T(8,128)(2,1)} %param.18) | data formatting | bytes 16777216 | tf_op jit(solution)/shard_map/reshape | solution.py:65
  61.9 18.4 %all-to-all-done = bf16[4,4,64,2048]{3,2,1,0:T(8,128)(2,1)} async-done(((bf16[4,4,64,2048]{3,2,1,0:T(8,128)(2,1)}), bf16[4,4,64,2048]{3,2,1,0:T(8,128)(2,1)}, u32[]{:S(2)}, u32[]{:S(2)}) %all-to-all-start) | async-done | bytes 4194336 | tf_op jit(solution)/shard_map/all_to_all | solution.py:44
  89.4 7.1 %multiply_reduce_fusion.1 = (f32[4,4,4,64]{3,1,2,0:T(4,128)S(1)}, f32[4,4,4,64,128]{4,3,1,2,0:T(8,128)S(1)}) fusion(bf16[4,2048,4,128,1]{3,2,1,0,4:T(4,128)(2,1)} %bitcast.190, bf16[4,4,64,2048]{3,2,1,0:T(8,128)(2,1)} %all-to-all-done), kind=kOutput, calls=%fused_computation.73 | convolution fusion | flops 2148528128 | bytes 14696448 | tf_op jit(solution)/shard_map/smcd,mdhk->mhsck/dot_general | solution.py:56
  123.5 4.1 fusion.74
  129.4 4.9 fusion.40
  151.6 8.9 %convolution_bitcast_fusion.1 = f32[4,16,128,128]{3,2,0,1:T(8,128)} fusion(f32[16,4,64,256]{3,2,1,0:T(8,128)S(1)} %fusion.28, f32[16,4,64,128]{3,2,1,0:T(8,128)S(1)} %get-tuple-element.190, f32[16,4,64]{2,1,0:T(4,128)S(1)} %copy.133), kind=kOutput, calls=%fused_computation.48 | convolution fusion | flops 805830656 | bytes 8421376 | tf_op jit(solution)/shard_map/bnik,bniv->bnkv/dot_general | solution.py:112
  160.6 12.0 %bitcast_subtract_fusion = f32[4,16,128,128]{3,2,0,1:T(8,128)} fusion(f32[128,128]{1,0:T(8,128)S(1)} %fusion.107, f32[4,16]{0,1:T(8,128)S(1)} %copy.127, f32[16,4,64,256]{3,2,1,0:T(8,128)} %copy-done.4, f32[16,4,64,128]{3,2,1,0:T(8,128)} %copy-done.2, f32[16,4,64]{2,1,0:T(4,128)S(1)} %copy.133), kind=kOutput, calls=%fused_computation.41 | convolution fusion | flops 807927808 | bytes 8470784 | tf_op jit(solution)/shard_map/bnik,bnil->bnkl/dot_general | solution.py:109
  173.7 43.9 %while.30 = (s32[]{:T(128)}, f32[16,128,128]{2,1,0:T(8,128)}, f32[16,128,128]{2,1,0:T(8,128)S(1)}, f32[4,16,64,128]{3,2,0,1:T(8,128)}, f32[4,16,64,128]{3,2,0,1:...) while((s32[]{:T(128)}, f32[16,128,128]{2,1,0:T(8,128)}, ...), condition=%wide.region_9.10_spmd.clone, body=%wide.region_8.9_spmd.clone.sunk | while | flops 1208877056 | bytes 37227696 | solution.py:138
  218.6 387.3 %while.29 = (s32[]{:T(128)}, f32[16,128,128]{2,1,0:T(8,128)}, f32[16,128,128]{2,1,0:T(8,128)}, f32[16,128,128]{2,1,0:T(8,128)}, f32[16,128,128]{2,1,0:T(8,128)S(1)}, /*index=5*/s32[]{:T(128)}) while((s32[]{:T(128)}, f32[16,128,128]{2,1,0:T(8,128)}, f32[16,128,128]{2,1,0:T(8,128)}, f32[16,128,128]{2,1,0:T(8,128)}, ...), condition=%wide.region_11.12_spmd, body=%wide.region_10.11_spmd.sunk | while | flops 402915328 | bytes 8388717 | solution.py:150
  221.7 24.1 %collective-permute-done = f32[16,128,128]{2,1,0:T(8,128)} collective-permute-done((f32[16,128,128]{2,1,0:T(8,128)}, f32[16,128,128]{2,1,0:T(8,128)}, u32[]{:S(2)}, u32[]{:S(2)}) %collective-permute-start) | collective-permute-done | bytes 1048608 | tf_op jit(solution)/shard_map/while/body/eval_jaxpr/ppermute | solution.py:12
  251.4 24.4 %collective-permute-done = f32[16,128,128]{2,1,0:T(8,128)} collective-permute-done((f32[16,128,128]{2,1,0:T(8,128)}, f32[16,128,128]{2,1,0:T(8,128)}, u32[]{:S(2)}, u32[]{:S(2)}) %collective-permute-start) | collective-permute-done | bytes 1048608 | tf_op jit(solution)/shard_map/while/body/eval_jaxpr/ppermute | solution.py:12
  281.5 23.6 %collective-permute-done = f32[16,128,128]{2,1,0:T(8,128)} collective-permute-done((f32[16,128,128]{2,1,0:T(8,128)}, f32[16,128,128]{2,1,0:T(8,128)}, u32[]{:S(2)}, u32[]{:S(2)}) %collective-permute-start) | collective-permute-done | bytes 1048608 | tf_op jit(solution)/shard_map/while/body/eval_jaxpr/ppermute | solution.py:12
  310.8 22.7 %collective-permute-done = f32[16,128,128]{2,1,0:T(8,128)} collective-permute-done((f32[16,128,128]{2,1,0:T(8,128)}, f32[16,128,128]{2,1,0:T(8,128)}, u32[]{:S(2)}, u32[]{:S(2)}) %collective-permute-start) | collective-permute-done | bytes 1048608 | tf_op jit(solution)/shard_map/while/body/eval_jaxpr/ppermute | solution.py:12
  339.1 21.9 %collective-permute-done = f32[16,128,128]{2,1,0:T(8,128)} collective-permute-done((f32[16,128,128]{2,1,0:T(8,128)}, f32[16,128,128]{2,1,0:T(8,128)}, u32[]{:S(2)}, u32[]{:S(2)}) %collective-permute-start) | collective-permute-done | bytes 1048608 | tf_op jit(solution)/shard_map/while/body/eval_jaxpr/ppermute | solution.py:12
  366.7 21.0 %collective-permute-done = f32[16,128,128]{2,1,0:T(8,128)} collective-permute-done((f32[16,128,128]{2,1,0:T(8,128)}, f32[16,128,128]{2,1,0:T(8,128)}, u32[]{:S(2)}, u32[]{:S(2)}) %collective-permute-start) | collective-permute-done | bytes 1048608 | tf_op jit(solution)/shard_map/while/body/eval_jaxpr/ppermute | solution.py:12
  393.3 20.2 %collective-permute-done = f32[16,128,128]{2,1,0:T(8,128)} collective-permute-done((f32[16,128,128]{2,1,0:T(8,128)}, f32[16,128,128]{2,1,0:T(8,128)}, u32[]{:S(2)}, u32[]{:S(2)}) %collective-permute-start) | collective-permute-done | bytes 1048608 | tf_op jit(solution)/shard_map/while/body/eval_jaxpr/ppermute | solution.py:12
  419.1 19.3 %collective-permute-done = f32[16,128,128]{2,1,0:T(8,128)} collective-permute-done((f32[16,128,128]{2,1,0:T(8,128)}, f32[16,128,128]{2,1,0:T(8,128)}, u32[]{:S(2)}, u32[]{:S(2)}) %collective-permute-start) | collective-permute-done | bytes 1048608 | tf_op jit(solution)/shard_map/while/body/eval_jaxpr/ppermute | solution.py:12
  444.1 18.5 %collective-permute-done = f32[16,128,128]{2,1,0:T(8,128)} collective-permute-done((f32[16,128,128]{2,1,0:T(8,128)}, f32[16,128,128]{2,1,0:T(8,128)}, u32[]{:S(2)}, u32[]{:S(2)}) %collective-permute-start) | collective-permute-done | bytes 1048608 | tf_op jit(solution)/shard_map/while/body/eval_jaxpr/ppermute | solution.py:12
  468.2 17.6 %collective-permute-done = f32[16,128,128]{2,1,0:T(8,128)} collective-permute-done((f32[16,128,128]{2,1,0:T(8,128)}, f32[16,128,128]{2,1,0:T(8,128)}, u32[]{:S(2)}, u32[]{:S(2)}) %collective-permute-start) | collective-permute-done | bytes 1048608 | tf_op jit(solution)/shard_map/while/body/eval_jaxpr/ppermute | solution.py:12
  491.4 16.7 %collective-permute-done = f32[16,128,128]{2,1,0:T(8,128)} collective-permute-done((f32[16,128,128]{2,1,0:T(8,128)}, f32[16,128,128]{2,1,0:T(8,128)}, u32[]{:S(2)}, u32[]{:S(2)}) %collective-permute-start) | collective-permute-done | bytes 1048608 | tf_op jit(solution)/shard_map/while/body/eval_jaxpr/ppermute | solution.py:12
  513.8 16.1 %collective-permute-done = f32[16,128,128]{2,1,0:T(8,128)} collective-permute-done((f32[16,128,128]{2,1,0:T(8,128)}, f32[16,128,128]{2,1,0:T(8,128)}, u32[]{:S(2)}, u32[]{:S(2)}) %collective-permute-start) | collective-permute-done | bytes 1048608 | tf_op jit(solution)/shard_map/while/body/eval_jaxpr/ppermute | solution.py:12
  535.6 17.3 %collective-permute-done = f32[16,128,128]{2,1,0:T(8,128)} collective-permute-done((f32[16,128,128]{2,1,0:T(8,128)}, f32[16,128,128]{2,1,0:T(8,128)}, u32[]{:S(2)}, u32[]{:S(2)}) %collective-permute-start) | collective-permute-done | bytes 1048608 | tf_op jit(solution)/shard_map/while/body/eval_jaxpr/ppermute | solution.py:12
  558.5 18.4 %collective-permute-done = f32[16,128,128]{2,1,0:T(8,128)} collective-permute-done((f32[16,128,128]{2,1,0:T(8,128)}, f32[16,128,128]{2,1,0:T(8,128)}, u32[]{:S(2)}, u32[]{:S(2)}) %collective-permute-start) | collective-permute-done | bytes 1048608 | tf_op jit(solution)/shard_map/while/body/eval_jaxpr/ppermute | solution.py:12
  582.6 19.6 %collective-permute-done = f32[16,128,128]{2,1,0:T(8,128)} collective-permute-done((f32[16,128,128]{2,1,0:T(8,128)}, f32[16,128,128]{2,1,0:T(8,128)}, u32[]{:S(2)}, u32[]{:S(2)}) %collective-permute-start) | collective-permute-done | bytes 1048608 | tf_op jit(solution)/shard_map/while/body/eval_jaxpr/ppermute | solution.py:12
  605.9 4.9 multiply_reduce_fusion
  619.6 9.6 %all-to-all-done.2 = bf16[4,4,64,512]{3,2,1,0:T(8,128)(2,1)S(1)} async-done(((bf16[4,4,64,512]{3,2,1,0:T(8,128)(2,1)}), bf16[4,4,64,512]{3,2,1,0:T(8,128)(2,1)S(1)}, u32[]{:S(2)}, u32[]{:S(2)}) %all-to-all-start.2) | async-done | bytes 1048608 | tf_op jit(solution)/shard_map/all_to_all | solution.py:164
  631.9 4.2 fusion.125
  636.1 28.5 %reduce-scatter.2.cloned.1.call-done = f32[256,2048]{1,0:T(8,128)} async-done(((f32[512,2048]{1,0:T(8,128)}), f32[256,2048]{1,0:T(8,128)}) %reduce-scatter.2.cloned.1.call-update) | async-done | bytes 2097168 | tf_op jit(solution)/shard_map/reduce_scatter | solution.py:167
  (175 shorter events, 213.0 us)
Async XLA Ops:
  6.5 625.3 %copy-start = (bf16[512,2048]{1,0:T(8,128)(2,1)S(1)}, bf16[512,2048]{1,0:T(8,128)(2,1)}, u32[]{:S(2)}) copy-start(bf16[512,2048]{1,0:T(8,128)(2,1)} %param.23) | copy-start | bytes 6291460
  14.8 12.3 %all-to-all-start.1 = ((bf16[4,2,128]{2,1,0:T(2,128)(2,1)}), bf16[4,2,128]{2,1,0:T(2,128)(2,1)S(1)}, u32[]{:S(2)}, u32[]{:S(2)}) async-start(bf16[4,2,128]{2,1,0:T(2,128)(2,1)} %reshape.258), calls=%async_computation.1 | async-start | bytes 4096 | tf_op jit(solution)/shard_map/all_to_all | solution.py:45
  27.0 5.3 copy-start.7
  27.0 53.2 %all-to-all-start = ((bf16[4,4,64,2048]{3,2,1,0:T(8,128)(2,1)}), bf16[4,4,64,2048]{3,2,1,0:T(8,128)(2,1)}, u32[]{:S(2)}, u32[]{:S(2)}) async-start(bf16[4,4,64,2048]{3,2,1,0:T(8,128)(2,1)} %bitcast.186), calls=%async_computation | async-start | bytes 8388608 | tf_op jit(solution)/shard_map/all_to_all | solution.py:44
  57.5 22.8 %copy-start.8 = (bf16[4,2048,4]{1,2,0:T(4,128)(2,1)S(1)}, bf16[4,2048,4]{1,2,0:T(4,128)(2,1)}, u32[]{:S(2)}) copy-start(bf16[4,2048,4]{1,2,0:T(4,128)(2,1)} %param.20) | copy-start | bytes 196612
  61.9 23.5 %copy-start.9 = (bf16[4,2048,4]{1,2,0:T(4,128)(2,1)S(1)}, bf16[4,2048,4]{1,2,0:T(4,128)(2,1)}, u32[]{:S(2)}) copy-start(bf16[4,2048,4]{1,2,0:T(4,128)(2,1)} %param.19) | copy-start | bytes 196612
  98.7 52.9 %copy-start.2 = (f32[16,4,64,128]{3,2,1,0:T(8,128)}, f32[16,4,64,128]{3,2,1,0:T(8,128)S(1)}, u32[]{:S(2)}) copy-start(f32[16,4,64,128]{3,2,1,0:T(8,128)S(1)} %get-tuple-element.190) | copy-start | bytes 6291460
  116.2 7.3 %slice-start = ((s8[8388608]{0:T(1024)(128)(4,1)}), s8[4194304]{0:T(1024)(128)(4,1)S(1)}, s32[]{:S(2)}) async-start(s8[8388608]{0:T(1024)(128)(4,1)} %bitcast.187), calls=%async_computation.5 | async-start | bytes 8388608
  118.5 5.0 slice-start.1
  144.2 7.4 %copy-start.4 = (f32[16,4,64,256]{3,2,1,0:T(8,128)}, f32[16,4,64,256]{3,2,1,0:T(8,128)S(1)}, u32[]{:S(2)}) copy-start(f32[16,4,64,256]{3,2,1,0:T(8,128)S(1)} %fusion.28) | copy-start | bytes 12582916
  173.9 3.3 copy-start.3
  184.8 3.3 copy-start.3
  195.7 3.3 copy-start.3
  206.6 3.3 copy-start.3
  218.6 27.2 %collective-permute-start = (f32[16,128,128]{2,1,0:T(8,128)}, f32[16,128,128]{2,1,0:T(8,128)}, u32[]{:S(2)}, u32[]{:S(2)}) collective-permute-start(f32[16,128,128]{2,1,0:T(8,128)} %get-tuple-element.328), channel_id=1, source_target_pairs={{0,8},{8,16},{16,24},{24,32},{32,40},{40,48},{48,56},{56,64},{64,7... | collective-permute-start | bytes 3145736 | tf_op jit(solution)/shard_map/while/body/eval_jaxpr/ppermute | solution.py:12
  249.5 26.4 %collective-permute-start = (f32[16,128,128]{2,1,0:T(8,128)}, f32[16,128,128]{2,1,0:T(8,128)}, u32[]{:S(2)}, u32[]{:S(2)}) collective-permute-start(f32[16,128,128]{2,1,0:T(8,128)} %get-tuple-element.328), channel_id=1, source_target_pairs={{0,8},{8,16},{16,24},{24,32},{32,40},{40,48},{48,56},{56,64},{64,7... | collective-permute-start | bytes 3145736 | tf_op jit(solution)/shard_map/while/body/eval_jaxpr/ppermute | solution.py:12
  279.6 25.5 %collective-permute-start = (f32[16,128,128]{2,1,0:T(8,128)}, f32[16,128,128]{2,1,0:T(8,128)}, u32[]{:S(2)}, u32[]{:S(2)}) collective-permute-start(f32[16,128,128]{2,1,0:T(8,128)} %get-tuple-element.328), channel_id=1, source_target_pairs={{0,8},{8,16},{16,24},{24,32},{32,40},{40,48},{48,56},{56,64},{64,7... | collective-permute-start | bytes 3145736 | tf_op jit(solution)/shard_map/while/body/eval_jaxpr/ppermute | solution.py:12
  308.8 24.6 %collective-permute-start = (f32[16,128,128]{2,1,0:T(8,128)}, f32[16,128,128]{2,1,0:T(8,128)}, u32[]{:S(2)}, u32[]{:S(2)}) collective-permute-start(f32[16,128,128]{2,1,0:T(8,128)} %get-tuple-element.328), channel_id=1, source_target_pairs={{0,8},{8,16},{16,24},{24,32},{32,40},{40,48},{48,56},{56,64},{64,7... | collective-permute-start | bytes 3145736 | tf_op jit(solution)/shard_map/while/body/eval_jaxpr/ppermute | solution.py:12
  337.2 23.8 %collective-permute-start = (f32[16,128,128]{2,1,0:T(8,128)}, f32[16,128,128]{2,1,0:T(8,128)}, u32[]{:S(2)}, u32[]{:S(2)}) collective-permute-start(f32[16,128,128]{2,1,0:T(8,128)} %get-tuple-element.328), channel_id=1, source_target_pairs={{0,8},{8,16},{16,24},{24,32},{32,40},{40,48},{48,56},{56,64},{64,7... | collective-permute-start | bytes 3145736 | tf_op jit(solution)/shard_map/while/body/eval_jaxpr/ppermute | solution.py:12
  364.7 22.9 %collective-permute-start = (f32[16,128,128]{2,1,0:T(8,128)}, f32[16,128,128]{2,1,0:T(8,128)}, u32[]{:S(2)}, u32[]{:S(2)}) collective-permute-start(f32[16,128,128]{2,1,0:T(8,128)} %get-tuple-element.328), channel_id=1, source_target_pairs={{0,8},{8,16},{16,24},{24,32},{32,40},{40,48},{48,56},{56,64},{64,7... | collective-permute-start | bytes 3145736 | tf_op jit(solution)/shard_map/while/body/eval_jaxpr/ppermute | solution.py:12
  391.4 22.1 %collective-permute-start = (f32[16,128,128]{2,1,0:T(8,128)}, f32[16,128,128]{2,1,0:T(8,128)}, u32[]{:S(2)}, u32[]{:S(2)}) collective-permute-start(f32[16,128,128]{2,1,0:T(8,128)} %get-tuple-element.328), channel_id=1, source_target_pairs={{0,8},{8,16},{16,24},{24,32},{32,40},{40,48},{48,56},{56,64},{64,7... | collective-permute-start | bytes 3145736 | tf_op jit(solution)/shard_map/while/body/eval_jaxpr/ppermute | solution.py:12
  417.2 21.2 %collective-permute-start = (f32[16,128,128]{2,1,0:T(8,128)}, f32[16,128,128]{2,1,0:T(8,128)}, u32[]{:S(2)}, u32[]{:S(2)}) collective-permute-start(f32[16,128,128]{2,1,0:T(8,128)} %get-tuple-element.328), channel_id=1, source_target_pairs={{0,8},{8,16},{16,24},{24,32},{32,40},{40,48},{48,56},{56,64},{64,7... | collective-permute-start | bytes 3145736 | tf_op jit(solution)/shard_map/while/body/eval_jaxpr/ppermute | solution.py:12
  442.2 20.4 %collective-permute-start = (f32[16,128,128]{2,1,0:T(8,128)}, f32[16,128,128]{2,1,0:T(8,128)}, u32[]{:S(2)}, u32[]{:S(2)}) collective-permute-start(f32[16,128,128]{2,1,0:T(8,128)} %get-tuple-element.328), channel_id=1, source_target_pairs={{0,8},{8,16},{16,24},{24,32},{32,40},{40,48},{48,56},{56,64},{64,7... | collective-permute-start | bytes 3145736 | tf_op jit(solution)/shard_map/while/body/eval_jaxpr/ppermute | solution.py:12
  466.3 19.5 %collective-permute-start = (f32[16,128,128]{2,1,0:T(8,128)}, f32[16,128,128]{2,1,0:T(8,128)}, u32[]{:S(2)}, u32[]{:S(2)}) collective-permute-start(f32[16,128,128]{2,1,0:T(8,128)} %get-tuple-element.328), channel_id=1, source_target_pairs={{0,8},{8,16},{16,24},{24,32},{32,40},{40,48},{48,56},{56,64},{64,7... | collective-permute-start | bytes 3145736 | tf_op jit(solution)/shard_map/while/body/eval_jaxpr/ppermute | solution.py:12
  489.5 18.7 %collective-permute-start = (f32[16,128,128]{2,1,0:T(8,128)}, f32[16,128,128]{2,1,0:T(8,128)}, u32[]{:S(2)}, u32[]{:S(2)}) collective-permute-start(f32[16,128,128]{2,1,0:T(8,128)} %get-tuple-element.328), channel_id=1, source_target_pairs={{0,8},{8,16},{16,24},{24,32},{32,40},{40,48},{48,56},{56,64},{64,7... | collective-permute-start | bytes 3145736 | tf_op jit(solution)/shard_map/while/body/eval_jaxpr/ppermute | solution.py:12
  511.9 18.0 %collective-permute-start = (f32[16,128,128]{2,1,0:T(8,128)}, f32[16,128,128]{2,1,0:T(8,128)}, u32[]{:S(2)}, u32[]{:S(2)}) collective-permute-start(f32[16,128,128]{2,1,0:T(8,128)} %get-tuple-element.328), channel_id=1, source_target_pairs={{0,8},{8,16},{16,24},{24,32},{32,40},{40,48},{48,56},{56,64},{64,7... | collective-permute-start | bytes 3145736 | tf_op jit(solution)/shard_map/while/body/eval_jaxpr/ppermute | solution.py:12
  533.7 19.2 %collective-permute-start = (f32[16,128,128]{2,1,0:T(8,128)}, f32[16,128,128]{2,1,0:T(8,128)}, u32[]{:S(2)}, u32[]{:S(2)}) collective-permute-start(f32[16,128,128]{2,1,0:T(8,128)} %get-tuple-element.328), channel_id=1, source_target_pairs={{0,8},{8,16},{16,24},{24,32},{32,40},{40,48},{48,56},{56,64},{64,7... | collective-permute-start | bytes 3145736 | tf_op jit(solution)/shard_map/while/body/eval_jaxpr/ppermute | solution.py:12
  556.6 20.3 %collective-permute-start = (f32[16,128,128]{2,1,0:T(8,128)}, f32[16,128,128]{2,1,0:T(8,128)}, u32[]{:S(2)}, u32[]{:S(2)}) collective-permute-start(f32[16,128,128]{2,1,0:T(8,128)} %get-tuple-element.328), channel_id=1, source_target_pairs={{0,8},{8,16},{16,24},{24,32},{32,40},{40,48},{48,56},{56,64},{64,7... | collective-permute-start | bytes 3145736 | tf_op jit(solution)/shard_map/while/body/eval_jaxpr/ppermute | solution.py:12
  580.6 21.5 %collective-permute-start = (f32[16,128,128]{2,1,0:T(8,128)}, f32[16,128,128]{2,1,0:T(8,128)}, u32[]{:S(2)}, u32[]{:S(2)}) collective-permute-start(f32[16,128,128]{2,1,0:T(8,128)} %get-tuple-element.328), channel_id=1, source_target_pairs={{0,8},{8,16},{16,24},{24,32},{32,40},{40,48},{48,56},{56,64},{64,7... | collective-permute-start | bytes 3145736 | tf_op jit(solution)/shard_map/while/body/eval_jaxpr/ppermute | solution.py:12
  605.8 5.0 copy-start.6
  616.0 13.2 %all-to-all-start.2 = ((bf16[4,4,64,512]{3,2,1,0:T(8,128)(2,1)}), bf16[4,4,64,512]{3,2,1,0:T(8,128)(2,1)S(1)}, u32[]{:S(2)}, u32[]{:S(2)}) async-start(bf16[4,4,64,512]{3,2,1,0:T(8,128)(2,1)} %copy.158), calls=%async_computation.2 | async-start | bytes 2097152 | tf_op jit(solution)/shard_map/all_to_all | solution.py:164
  619.5 45.0 %reduce-scatter.2.cloned.1.call-start = ((), (), s32[]{:S(2)}) async-start(), calls=%async_computation.4 | async-start | bytes 6291456 | tf_op jit(solution)/shard_map/reduce_scatter | solution.py:167
  (5 other events, 11.5 us)
Sparse Core Ops, SparseCore 0:
  636.2 28.3 reduce-scatter.1
where the time goes:
time: 685 us; the launch traced here: 675 us
  waiting for transfers between devices  358 us (52%)
  matrix products  195 us (28%)
  local copies, waits for them, and re-layouts  53 us (8%)
  starting transfers between devices  43.6 us (6%)
  between operations  14.3 us (2%)
  other arithmetic  10.5 us (2%)
    ppermute x15, waiting for transfers between devices, shifted(): return lax.ppermute(shard, axis, pairs)  301 us
    dot_general x15, matrix products, forward_state_update(): jnp.einsum('bkl,blv->bkv', whole_map, incoming, precision=precise_result)  55.9 us
    ppermute x15, starting transfers between devices, shifted(): return lax.ppermute(shard, axis, pairs)  29.8 us
    reduce_scatter x1, waiting for transfers between devices, per_device(): lax.psum_scatter(jnp.dot(picked, w_out, preferred_element_type=jnp.float3...  28.5 us
    all_to_all x1, waiting for transfers between devices, per_device(): lax.all_to_all(outgoing, 'mem', split_axis=0, concat_axis=0, tiled=True)  18.4 us
  transfers between devices with their start and end apart: 19, of which 18 were waited for; matrix products, arithmetic and copies ran while one was open for 5% of the time, Pallas kernels for 0%

commit v1 on v0

v1 whole, which is shorter than its diff:
```python
import functools

import jax
import jax.numpy as jnp
from jax import lax
from jax.experimental import pallas as pl
from jax.experimental.pallas import tpu as pltpu
from jax.sharding import PartitionSpec as P

MESH = pl.DeviceIdType.MESH
F32 = jnp.float32
BF16 = jnp.bfloat16
CTX, MEM, HALF = 16, 4, 2
TOK = 512
D = 2048
DH = D // 2
CAP = 64
LOCAL = 4
HEADS = 4
ROWS = MEM * CAP
K = 128


def mm(a, b):
    return jnp.dot(a, b, preferred_element_type=F32)


def mm_nt(a, b):
    return lax.dot_general(a, b, (((1,), (1,)), ((), ())), preferred_element_type=F32)


def split(x):
    hi = x.astype(BF16)
    return hi, (x - hi.astype(F32)).astype(BF16)


def iota(shape, axis):
    return lax.broadcasted_iota(jnp.int32, shape, axis)


def dispatch_kernel(
    routes_ref, tok_ref, x_ref, cnt_ref, tok, outgoing, counts,
    tok_sem, own_sem, send_sem, recv_sem, csend_sem, crecv_sem, fsend_sem, frecv_sem,
):
    z = lax.axis_index("mem")
    h = lax.axis_index("half")
    load = pltpu.make_async_copy(
        tok_ref.at[:, pl.ds(pl.multiple_of(h * DH, DH), DH)], tok, tok_sem
    )
    load.start()
    barrier = pltpu.get_barrier_semaphore()
    for d in range(1, MEM):
        pl.semaphore_signal(
            barrier, inc=1, device_id={"mem": lax.rem(z + d, MEM)}, device_id_type=MESH
        )
    pl.semaphore_signal(barrier, inc=1, device_id={"half": 1 - h}, device_id_type=MESH)

    route = routes_ref[...]
    member = iota((MEM * LOCAL, TOK), 0) == route
    member_f = member.astype(F32)
    upper = (iota((TOK, TOK), 0) <= iota((TOK, TOK), 1)).astype(F32).astype(BF16)
    running = mm(member_f.astype(BF16), upper)
    place = jnp.sum(running * member_f, axis=0, keepdims=True).astype(jnp.int32) - 1
    slots = route * CAP + place
    totals = jnp.sum(member_f, axis=1, keepdims=True)
    counts[...] = jnp.zeros_like(counts)
    for to in range(MEM):
        counts[to, 0:LOCAL, :] = jnp.broadcast_to(
            totals[to * LOCAL : (to + 1) * LOCAL], (LOCAL, 128)
        )
    load.wait()
    for to in range(MEM):
        pick = (iota((ROWS, TOK), 0) + to * ROWS == slots).astype(F32).astype(BF16)
        outgoing[to] = mm(pick, tok[...]).astype(BF16).reshape(LOCAL, CAP, DH)

    pl.semaphore_wait(barrier, MEM)
    mine = pl.ds(pl.multiple_of(h * DH, DH), DH)

    def rows_of(src):
        return pl.ds(pl.multiple_of(src * CAP, CAP), CAP)

    own = pltpu.make_async_copy(outgoing.at[z], x_ref.at[:, rows_of(z), mine], own_sem.at[0])
    own.start()
    own_cnt = pltpu.make_async_copy(counts.at[z], cnt_ref.at[z], own_sem.at[1])
    own_cnt.start()
    sends = []
    for d in (2, 1, 3):
        to = lax.rem(z + d, MEM)
        cnt = pltpu.make_async_remote_copy(
            counts.at[to], cnt_ref.at[z], csend_sem.at[d], crecv_sem.at[d],
            device_id={"mem": to}, device_id_type=MESH,
        )
        cnt.start()
        copy = pltpu.make_async_remote_copy(
            outgoing.at[to], x_ref.at[:, rows_of(z), mine], send_sem.at[d], recv_sem.at[d],
            device_id={"mem": to}, device_id_type=MESH,
        )
        copy.start()
        sends += [cnt, copy]
    forward = pltpu.make_async_remote_copy(
        outgoing.at[z], x_ref.at[:, rows_of(z), mine], fsend_sem.at[0], frecv_sem.at[0],
        device_id={"half": 1 - h}, device_id_type=MESH,
    )
    forward.start()
    forwards = [forward]
    for d in (1, 3, 2):
        src = lax.rem(z + MEM - d, MEM)
        landed = x_ref.at[:, rows_of(src), mine]
        pltpu.make_async_remote_copy(
            outgoing.at[z], landed, send_sem.at[d], recv_sem.at[d],
            device_id={"mem": src}, device_id_type=MESH,
        ).wait_recv()
        forward = pltpu.make_async_remote_copy(
            landed, landed, fsend_sem.at[d], frecv_sem.at[d],
            device_id={"half": 1 - h}, device_id_type=MESH,
        )
        forward.start()
        forwards.append(forward)
        pltpu.make_async_remote_copy(
            counts.at[z], cnt_ref.at[src], csend_sem.at[d], crecv_sem.at[d],
            device_id={"mem": src}, device_id_type=MESH,
        ).wait_recv()
    for copy in sends:
        copy.wait_send()
    own.wait()
    own_cnt.wait()
    for copy in forwards:
        copy.wait()


def dispatch(routes, tokens):
    dma = pltpu.SemaphoreType.DMA
    return pl.pallas_call(
        dispatch_kernel,
        name="dispatch",
        out_shape=(
            jax.ShapeDtypeStruct((LOCAL, ROWS, D), BF16),
            jax.ShapeDtypeStruct((MEM, 8, 128), F32),
        ),
        in_specs=[pl.BlockSpec(memory_space=pltpu.VMEM), pl.BlockSpec(memory_space=pl.ANY)],
        out_specs=(pl.BlockSpec(memory_space=pl.ANY), pl.BlockSpec(memory_space=pl.ANY)),
        scratch_shapes=[
            pltpu.VMEM((TOK, DH), BF16),
            pltpu.VMEM((MEM, LOCAL, CAP, DH), BF16),
            pltpu.VMEM((MEM, 8, 128), F32),
            dma, dma((2,)), dma((MEM,)), dma((MEM,)), dma((MEM,)), dma((MEM,)),
            dma((MEM,)), dma((MEM,)),
        ],
        compiler_params=pltpu.CompilerParams(collective_id=0, has_side_effects=True),
    )(routes.reshape(1, TOK), tokens)


def local_kernel(
    rate_ref, cnt_ref, x_ref, wk_ref, wv_ref, wq_ref, wb_ref, wd_ref,
    mw_ref, base_ref, reach_ref, gates,
):
    m = pl.program_id(0)
    x = x_ref[0]
    gates[...] = jnp.zeros_like(gates)
    gates[:, 0:HEADS] = wb_ref[0]
    gates[:, HEADS : 2 * HEADS] = wd_ref[0]
    logits = mm(x, gates[...])
    keys_all = mm(x, wk_ref[0])
    values_all = mm(x, wv_ref[0])
    query_all = mm(x, wq_ref[...])

    lane = iota((1, 128), 1)
    rate = jnp.zeros((1, 128), F32)
    for h in range(HEADS):
        rate = jnp.where(lane == HEADS + h, rate_ref[m, h], rate)
    live = (
        iota((MEM, CAP, 128), 1).astype(F32) < cnt_ref[:, pl.ds(m, 1), :]
    ).astype(F32).reshape(ROWS, 128)
    strength = jax.nn.sigmoid(logits) * live
    soft = jnp.maximum(logits, 0.0) + jnp.log1p(jnp.exp(-jnp.abs(logits)))
    forget = -rate * soft * live
    row, col = iota((ROWS, ROWS), 0), iota((ROWS, ROWS), 1)
    lower = row >= col
    apart = row ^ col
    tri = lower.astype(F32).astype(BF16)
    hi, mid = split(forget)
    low = (forget - hi.astype(F32) - mid.astype(F32)).astype(BF16)
    total = mm(tri, hi) + mm(tri, mid) + mm(tri, low)
    total_t = total.T

    heads = range(HEADS)
    keys, query, values, scores, mixing, inverse, grow, target, running = (
        [None] * HEADS for _ in range(9)
    )
    for h in heads:
        at = slice(h * K, (h + 1) * K)
        k = keys_all[:, at]
        q = query_all[:, at]
        k = k * lax.rsqrt(jnp.sum(k * k, axis=1, keepdims=True) + 1e-06)
        q = q * lax.rsqrt(jnp.sum(q * q, axis=1, keepdims=True) + 1e-06)
        keys[h], query[h], values[h] = k, q, values_all[:, at]
        k_hi, k_lo = split(k)
        q_hi, q_lo = split(q)
        left = jnp.concatenate(
            [jnp.concatenate([k_hi, k_lo], axis=1), jnp.concatenate([q_hi, q_lo], axis=1)], axis=0
        )
        both = mm_nt(left, jnp.concatenate([k_hi, k_hi], axis=1)) + mm_nt(
            jnp.concatenate([k_hi, q_hi], axis=0), k_lo
        )
        g_col = total[:, HEADS + h : HEADS + h + 1]
        g_row = total_t[HEADS + h : HEADS + h + 1, :]
        fade = jnp.where(lower, jnp.exp(jnp.where(lower, g_col - g_row, 0.0)), 0.0)
        beta = strength[:, h : h + 1]
        scores[h] = both[ROWS:] * fade
        mixing[h] = jnp.where(row > col, both[:ROWS] * fade * beta, 0.0)
        grow[h] = jnp.exp(g_col)
        running[h] = g_col
        target[h] = jnp.concatenate([(beta * grow[h]) * k, beta * values[h]], axis=1)
        inverse[h] = jnp.where(row == col, 1.0, jnp.where(apart == 1, -mixing[h], 0.0))
    size = 2
    while size < ROWS:
        half_way = [None] * HEADS
        for h in heads:
            part = jnp.where((apart >= size) & (apart < 2 * size), mixing[h], 0.0).astype(BF16)
            half_way[h] = mm(part, inverse[h].astype(BF16)).astype(BF16)
        for h in heads:
            inverse[h] = inverse[h] - mm(inverse[h].astype(BF16), half_way[h])
        size *= 2
    solved = [None] * HEADS
    for h in heads:
        inv = inverse[h].astype(BF16)
        guess = mm(inv, target[h].astype(BF16))
        a_hi, a_lo = split(mixing[h])
        g_hi, g_lo = split(guess)
        rest = target[h] - guess - (mm(a_hi, g_hi) + mm(a_lo, g_hi) + mm(a_hi, g_lo))
        solved[h] = guess + mm(inv, rest.astype(BF16))
    diagonal = iota((K, K), 0) == iota((K, K), 1)
    for h in heads:
        last = running[h][ROWS - 1 : ROWS, :]
        tail = keys[h] * jnp.exp(last - running[h])
        lhs = jnp.concatenate([scores[h], tail.T], axis=0)
        l_hi, l_lo = split(lhs)
        y_hi, y_lo = split(solved[h])
        out = mm(l_hi, y_hi) + mm(l_lo, y_hi) + mm(l_hi, y_lo)
        base_ref[0, :, h * K : (h + 1) * K] = out[:ROWS, K:]
        reach = query[h] * grow[h] - out[:ROWS, :K]
        r_hi, r_lo = split(reach)
        reach_ref[0, :, 2 * h * K : (2 * h + 1) * K] = r_hi
        reach_ref[0, :, (2 * h + 1) * K : (2 * h + 2) * K] = r_lo
        step = jnp.where(diagonal, jnp.exp(last), 0.0) - out[ROWS:, :K]
        mw_ref[h, :, :K] = step.astype(BF16)
        mw_ref[h, :, K:] = out[ROWS:, K:].astype(BF16)


def local_algebra(rate, counts, x, w_key, w_value, w_query, w_beta, w_decay):
    width = HEADS * K
    per_memory = lambda *block: pl.BlockSpec((1,) + block, lambda m: (m, 0, 0))
    return pl.pallas_call(
        local_kernel,
        name="local_algebra",
        grid=(LOCAL,),
        out_shape=(
            jax.ShapeDtypeStruct((LOCAL * HEADS, K, 2 * K), BF16),
            jax.ShapeDtypeStruct((LOCAL, ROWS, width), F32),
            jax.ShapeDtypeStruct((LOCAL, ROWS, 2 * width), BF16),
        ),
        in_specs=[
            pl.BlockSpec(memory_space=pltpu.SMEM),
            pl.BlockSpec((MEM, 8, 128), lambda m: (0, 0, 0)),
            per_memory(ROWS, D),
            per_memory(D, width),
            per_memory(D, width),
            pl.BlockSpec((D, width), lambda m: (0, 0)),
            per_memory(D, HEADS),
            per_memory(D, HEADS),
        ],
        out_specs=(
            pl.BlockSpec((HEADS, K, 2 * K), lambda m: (m, 0, 0)),
            per_memory(ROWS, width),
            per_memory(ROWS, 2 * width),
        ),
        scratch_shapes=[pltpu.VMEM((D, 128), BF16)],
        compiler_params=pltpu.CompilerParams(vmem_limit_bytes=60 * 1024 * 1024),
    )(rate, counts, x, w_key, w_value, w_query, w_beta, w_decay)


def exchange_kernel(
    routes_ref, mw_ref, base_ref, reach_ref, gain_ref, w_ref, out_ref,
    maps, states, entering, reply, returned, picked, partner, w_other,
    own_sem, map_send, map_recv, state_send, state_recv, ret_send, ret_recv,
    pair_send, pair_recv,
):
    c = lax.axis_index("ctx")
    z = lax.axis_index("mem")
    h = lax.axis_index("half")
    other = {"half": 1 - h}
    barrier = pltpu.get_barrier_semaphore()
    for d in range(1, CTX):
        pl.semaphore_signal(
            barrier, inc=1, device_id={"ctx": lax.rem(c + d, CTX)}, device_id_type=MESH
        )
    for d in range(1, MEM):
        pl.semaphore_signal(
            barrier, inc=1, device_id={"mem": lax.rem(z + d, MEM)}, device_id_type=MESH
        )
    pl.semaphore_signal(barrier, inc=1, device_id=other, device_id_type=MESH)
    pl.semaphore_wait(barrier, CTX - 1 + MEM)

    def map_copy(d):
        to = lax.rem(c + d, CTX)
        return pltpu.make_async_remote_copy(
            mw_ref.at[to], maps.at[c], map_send.at[d], map_recv.at[c],
            device_id={"ctx": to}, device_id_type=MESH,
        )

    @pl.when(c < CTX - 1)
    def _():
        for d in range(1, CTX):
            map_copy(d).start()

    own_map = pltpu.make_async_copy(mw_ref.at[c], maps.at[c], own_sem.at[0])
    own_map.start()
    w_copy = pltpu.make_async_remote_copy(
        w_ref, w_other, pair_send.at[0], pair_recv.at[0], device_id=other, device_id_type=MESH
    )
    w_copy.start()
    own_map.wait()

    def state_copy(to):
        return pltpu.make_async_remote_copy(
            states.at[to], entering.at[c], state_send.at[to], state_recv.at[c],
            device_id={"ctx": to}, device_id_type=MESH,
        )

    state = None
    for j in range(CTX - 1):

        @pl.when(c != j)
        def _():
            pltpu.make_async_remote_copy(
                mw_ref.at[j], maps.at[j], map_send.at[0], map_recv.at[j],
                device_id={"ctx": j}, device_id_type=MESH,
            ).wait_recv()

        add = maps[j, :, K:].astype(F32)
        if j == 0:
            state = add
        else:
            step = maps[j, :, :K]
            s_hi, s_lo = split(state)
            state = add + mm(
                jnp.concatenate([step, step], axis=1), jnp.concatenate([s_hi, s_lo], axis=0)
            )
        states[j + 1] = state.astype(BF16)

        @pl.when(c != j + 1)
        def _():
            state_copy(j + 1).start()

    @pl.when(c == 0)
    def _():
        entering[...] = jnp.zeros_like(entering)

    @pl.when(c > 0)
    def _():
        keep = pltpu.make_async_copy(states.at[c], entering.at[c], own_sem.at[0])
        keep.start()
        keep.wait()
        for d in range(1, CTX):
            src = lax.rem(c + d, CTX)
            pltpu.make_async_remote_copy(
                states.at[1], entering.at[src], state_send.at[0], state_recv.at[src],
                device_id={"ctx": src}, device_id_type=MESH,
            ).wait_recv()

    for m in range(LOCAL):
        for n in range(HEADS):
            at = slice(n * K, (n + 1) * K)
            s = entering[m * HEADS + n]
            heads_out = base_ref[m, :, at] + mm(
                reach_ref[m, :, 2 * n * K : (2 * n + 2) * K], jnp.concatenate([s, s], axis=0)
            )
            scale = lax.rsqrt(jnp.mean(heads_out * heads_out, axis=1, keepdims=True) + 1e-05)
            normed = (heads_out * scale * gain_ref[:, at]).astype(BF16)
            for src in range(MEM):
                reply[src, m * CAP : (m + 1) * CAP, at] = normed[src * CAP : (src + 1) * CAP]
    sends = []
    for d in (2, 1, 3):
        to = lax.rem(z + d, MEM)
        copy = pltpu.make_async_remote_copy(
            reply.at[to], returned.at[z], ret_send.at[d], ret_recv.at[d],
            device_id={"mem": to}, device_id_type=MESH,
        )
        copy.start()
        sends.append(copy)

    route = routes_ref[...]
    member_f = (iota((TOK, 128), 1) == route).astype(F32)
    lower = (iota((TOK, TOK), 0) >= iota((TOK, TOK), 1)).astype(F32).astype(BF16)
    running = mm(lower, member_f.astype(BF16))
    place = jnp.sum(running * member_f, axis=1, keepdims=True).astype(jnp.int32) - 1
    slots = route * CAP + place

    def pick(src, rows):
        chosen = (iota((TOK, ROWS), 1) + src * ROWS == slots).astype(F32).astype(BF16)
        return mm(chosen, rows)

    total = pick(z, reply[z])
    for d in (1, 3, 2):
        src = lax.rem(z + MEM - d, MEM)
        pltpu.make_async_remote_copy(
            reply.at[z], returned.at[src], ret_send.at[d], ret_recv.at[d],
            device_id={"mem": src}, device_id_type=MESH,
        ).wait_recv()
        total = total + pick(src, returned[src])
    picked[...] = total.astype(BF16)
    here = pl.ds(pl.multiple_of(h * (TOK // 2), TOK // 2), TOK // 2)
    there = pl.ds(pl.multiple_of((1 - h) * (TOK // 2), TOK // 2), TOK // 2)
    swap = pltpu.make_async_remote_copy(
        picked.at[there], partner, pair_send.at[1], pair_recv.at[1],
        device_id=other, device_id_type=MESH,
    )
    swap.start()
    mixed = mm(picked[here, :], w_ref[...])
    w_copy.wait()
    swap.wait()
    out_ref[...] = (mixed + mm(partner[...], w_other[...])).astype(BF16)
    for copy in sends:
        copy.wait_send()

    @pl.when(c < CTX - 1)
    def _():
        for d in range(1, CTX):
            map_copy(d).wait_send()

    for j in range(CTX - 1):

        @pl.when(c != j + 1)
        def _():
            state_copy(j + 1).wait_send()


def exchange(routes, mw, base, reach, gain, w_out):
    dma = pltpu.SemaphoreType.DMA
    width = HEADS * K
    return pl.pallas_call(
        exchange_kernel,
        name="exchange",
        out_shape=jax.ShapeDtypeStruct((TOK // 2, D), BF16),
        in_specs=[pl.BlockSpec(memory_space=pltpu.VMEM)] * 6,
        out_specs=pl.BlockSpec(memory_space=pltpu.VMEM),
        scratch_shapes=[
            pltpu.VMEM((CTX, K, 2 * K), BF16),
            pltpu.VMEM((CTX, K, K), BF16),
            pltpu.VMEM((CTX, K, K), BF16),
            pltpu.VMEM((MEM, ROWS, width), BF16),
            pltpu.VMEM((MEM, ROWS, width), BF16),
            pltpu.VMEM((TOK, width), BF16),
            pltpu.VMEM((TOK // 2, width), BF16),
            pltpu.VMEM((width, D), BF16),
            dma((1,)), dma((CTX,)), dma((CTX,)), dma((CTX,)), dma((CTX,)),
            dma((MEM,)), dma((MEM,)), dma((2,)), dma((2,)),
        ],
        compiler_params=pltpu.CompilerParams(
            collective_id=1, has_side_effects=True, vmem_limit_bytes=60 * 1024 * 1024
        ),
    )(routes, mw, base, reach, gain.reshape(1, width), w_out)


def per_device(
    tokens, routes, w_query, w_key, w_value, w_beta, w_decay, decay_rate, norm_gain, w_out
):
    x, counts = dispatch(routes, tokens)
    mw, base, reach = local_algebra(
        decay_rate, counts, x, w_key, w_value, w_query, w_beta, w_decay
    )
    return exchange(routes, mw, base, reach, norm_gain, w_out)


def solution(mesh):
    in_specs = (
        P(("ctx", "mem"), None),
        P(("ctx", "mem"), None),
        P(None, "half"),
        P("mem", None, "half"),
        P("mem", None, "half"),
        P("mem", None, "half"),
        P("mem", None, "half"),
        P("mem", "half"),
        P("half"),
        P("half", None),
    )
    out_specs = P(("ctx", "mem", "half"), None)
    return jax.shard_map(
        per_device, mesh=mesh, in_specs=in_specs, out_specs=out_specs, check_vma=False
    )
```

time: 685 us -> 134 us (0.20); the launches traced: 675 us -> 133 us
  waiting for transfers between devices: 358 us -> 0 us
  matrix products: 195 us -> 0 us
  Pallas kernels: 0 us -> 126 us
  local copies, waits for them, and re-layouts: 53 us -> 6.83 us
  starting transfers between devices: 43.6 us -> 0 us
  between operations: 14.3 us -> 0.04 us
  other arithmetic: 10.5 us -> 0 us
    ppermute x15 -> x0, waiting for transfers between devices: 301 us -> none  [shifted(): return lax.ppermute(shard, axis, pairs)]
    dot_general x55 -> x0, matrix products: 195 us -> none  [the longest x15 55.9 us: forward_state_update(): jnp.einsum('bkl,blv->bkv', whole_map, incoming, precision=precise_result)]
    pallas_call x0 -> x3, Pallas kernels: none -> 126 us  [the longest x1 50.4 us: exchange(): pl.pallas_call(exchange_kernel, name='exchange', out_shape=jax.ShapeDtype...]
    ppermute x15 -> x0, starting transfers between devices: 29.8 us -> none  [shifted(): return lax.ppermute(shard, axis, pairs)]
    reshape x4 -> x0, local copies, waits for them, and re-layouts: 29.2 us -> none  [the longest x1 12.5 us: per_device(): w_value.reshape(mem_local, width, heads_here, value_size)]
    reduce_scatter x1 -> x0, waiting for transfers between devices: 28.5 us -> none  [per_device(): lax.psum_scatter(jnp.dot(picked, w_out, preferred_element_type=jnp.float3...]
    all_to_all x3 -> x0, waiting for transfers between devices: 28 us -> none  [the longest x1 18.4 us: per_device(): lax.all_to_all(outgoing, 'mem', split_axis=0, concat_axis=0, tiled=True)]
    all_to_all x3 -> x0, starting transfers between devices: 13.7 us -> none  [the longest x1 5.21 us: per_device(): lax.all_to_all(outgoing, 'mem', split_axis=0, concat_axis=0, tiled=True)]
  transfers between devices with their start and end apart: 19 -> 0, of which waited for: 18 -> 0; matrix products, arithmetic and copies ran while one was open for 5% -> 0% of each run, Pallas kernels for 0% -> 0%
where the time goes in v1:
time: 134 us; the launch traced here: 133 us
  Pallas kernels  126 us (94%)
  local copies, waits for them, and re-layouts  6.83 us (5%)
    pallas_call x1, Pallas kernels, exchange(): pl.pallas_call(exchange_kernel, name='exchange', out_shape=jax.ShapeDtype...  50.4 us
    pallas_call x1, Pallas kernels, local_algebra(): pl.pallas_call(local_kernel, name='local_algebra', grid=(LOCAL,), out_sha...  41.2 us
    pallas_call x1, Pallas kernels, dispatch(): pl.pallas_call(dispatch_kernel, name='dispatch', out_shape=(jax.ShapeDtyp...  34.7 us
    unnamed x10, local copies, waits for them, and re-layouts  6.83 us

profile of v1, /device:TPU:25, one launch (start us, length us, event | category | flops | bytes accessed | tf_op | source)
XLA Modules:
  0.0 133.2 jit_solution(4053857732298838774)
XLA Ops:
  0.0 0.0 copy-start
  0.0 0.0 copy-start.1
  0.0 34.7 %dispatch.1 = (bf16[4,256,2048]{2,1,0:T(8,128)(2,1)}, f32[4,8,128]{2,1,0:T(8,128)}) custom-call(s32[1,512]{1,0:T(1,128)} %bitcast.2, bf16[512,2048]{1,0:T(8,128)(2,1)} %tok_ref.1), custom_call_target="tpu_custom_call" | custom-call | tf_op jit(solution)/shard_map/dispatch/pallas_call | solution.py:133
  34.7 0.0 copy-done
  34.7 1.8 %copy.11.wb_ref = bf16[4,2048,4]{2,1,0:T(8,128)(2,1)} copy(bf16[4,2048,4]{1,2,0:T(4,128)(2,1)S(1)} %copy-done) | data formatting | bytes 131072 | tf_op args[5]
  36.5 0.0 copy-done.1
  36.5 1.8 %copy.12.wd_ref = bf16[4,2048,4]{2,1,0:T(8,128)(2,1)} copy(bf16[4,2048,4]{1,2,0:T(4,128)(2,1)S(1)} %copy-done.1) | data formatting | bytes 131072 | tf_op args[6]
  38.4 0.0 copy-start.2
  38.4 41.2 %local_algebra.1 = (bf16[16,128,256]{2,1,0:T(8,128)(2,1)}, f32[4,256,512]{2,1,0:T(8,128)}, bf16[4,256,1024]{2,1,0:T(8,128)(2,1)}) custom-call(f32[4,4]{1,0:T(4,128)} %rate_ref.1, f32[4,8,128]{2,1,0:T(8,128)} %get-tuple-element.10.cnt_ref, bf16[4,256,2048]{2,1,0:T(8,128)(2,1)} %get-tuple-element.11.x_ref, bf16[4,2048,512]{2,1,0:T(8,128)(2,1)} %wk_ref.1, ...), custom_call_target="tpu_custom_call" | custom-call | tf_op jit(solution)/shard_map/local_algebra/pallas_call | solution.py:253
  79.6 0.0 copy-done.2
  79.6 0.9 copy.13.routes_ref
  80.5 50.4 %exchange.1 = bf16[256,2048]{1,0:T(8,128)(2,1)} custom-call(s32[512,1]{1,0:T(8,128)} %copy.13.routes_ref, bf16[16,128,256]{2,1,0:T(8,128)(2,1)} %get-tuple-element.12.mw_ref, f32[4,256,512]{2,1,0:T(8,128)} %get-tuple-element.13.base_ref, bf16[4,256,1024]{2,1,0:T(8,128)(2,1)} %get-tuple-element.14.reach_ref, f32[1,512]{1,0:T(1,128)} %bitcast.3, ...), custom_call_target="tpu_custom_call" | custom-call | tf_op jit(solution)/shard_map/exchange/pallas_call | solution.py:441
  130.8 2.3 %copy.15 = bf16[256,2048]{1,0:T(8,128)(2,1)} copy(bf16[256,2048]{1,0:T(8,128)(2,1)} %exchange.1) | data formatting | bytes 2097152
Async XLA Ops:
  0.0 34.7 %copy-start = (bf16[4,2048,4]{1,2,0:T(4,128)(2,1)S(1)}, bf16[4,2048,4]{1,2,0:T(4,128)(2,1)}, u32[]{:S(2)}) copy-start(bf16[4,2048,4]{1,2,0:T(4,128)(2,1)} %param.15) | copy-start | bytes 196612
  0.0 36.5 %copy-start.1 = (bf16[4,2048,4]{1,2,0:T(4,128)(2,1)S(1)}, bf16[4,2048,4]{1,2,0:T(4,128)(2,1)}, u32[]{:S(2)}) copy-start(bf16[4,2048,4]{1,2,0:T(4,128)(2,1)} %param.16) | copy-start | bytes 196612
  38.4 41.2 %copy-start.2 = (s32[512,1]{0,1:T(1,128)S(1)}, s32[512,1]{0,1:T(1,128)}, u32[]{:S(2)}) copy-start(s32[512,1]{0,1:T(1,128)} %param.11) | copy-start | bytes 6148

commit v2 on v0

v2 whole, which is shorter than its diff:
```python
import jax
import jax.numpy as jnp
from jax import lax
from jax.experimental import pallas as pl
from jax.experimental.pallas import tpu as pltpu
from jax.sharding import PartitionSpec as P

MESH = pl.DeviceIdType.MESH
F32 = jnp.float32
BF16 = jnp.bfloat16
CTX, MEM = 16, 4
TOK = 512
D = 2048
DH = D // 2
CAP = 64
LOCAL = 4
HEADS = 4
ROWS = MEM * CAP
K = 128
WIDTH = HEADS * K


def mm(a, b):
    return jnp.dot(a, b, preferred_element_type=F32)


def mm_nt(a, b):
    return lax.dot_general(a, b, (((1,), (1,)), ((), ())), preferred_element_type=F32)


def split(x):
    hi = x.astype(BF16)
    return hi, (x - hi.astype(F32)).astype(BF16)


def iota(shape, axis):
    return lax.broadcasted_iota(jnp.int32, shape, axis)


def ones_where(mask):
    return mask.astype(F32).astype(BF16)


def aligned(index, size):
    return pl.ds(pl.multiple_of(index * size, size), size)


def unit(x):
    return x * lax.rsqrt(jnp.sum(x * x, axis=1, keepdims=True) + 1e-06)


def level_rows(x, size):
    return jnp.concatenate(
        [x[at + size : at + 2 * size] for at in range(0, ROWS, 2 * size)], axis=0
    )


def spread_rows(x, size):
    gap = jnp.zeros((size, x.shape[1]), x.dtype)
    parts = []
    for at in range(0, ROWS // 2, size):
        parts += [gap, x[at : at + size]]
    return jnp.concatenate(parts, axis=0)


def layer_kernel(
    rate_ref, routes_ref, tok_ref, wq_ref, wk_ref, wv_ref, wb_ref, wd_ref, gain_ref, wo_ref,
    out_ref,
    tok, outgoing, counts, cnt, xbuf, wq, wk, wv, gates, total_s, total_ts, keys_s, solved_hi,
    solved_lo, mw, maps, states, entering, base, reach, reply, returned, picked, partner, wo,
    w_other,
    load_sem, wkv_sem, own_sem, x_send, x_recv, c_send, c_recv, f_send, f_recv,
    map_send, map_recv, state_send, state_recv, ret_send, ret_recv, pair_send, pair_recv,
):
    c = lax.axis_index("ctx")
    z = lax.axis_index("mem")
    half = lax.axis_index("half")
    other = {"half": 1 - half}
    mine = aligned(half, DH)
    heads = range(HEADS)

    tok_load = pltpu.make_async_copy(tok_ref.at[:, mine], tok, load_sem.at[0])
    tok_load.start()
    barrier = pltpu.get_barrier_semaphore()
    for d in range(1, MEM):
        pl.semaphore_signal(
            barrier, inc=1, device_id={"mem": lax.rem(z + d, MEM)}, device_id_type=MESH
        )
    pl.semaphore_signal(barrier, inc=1, device_id=other, device_id_type=MESH)
    for d in range(1, CTX):
        pl.semaphore_signal(
            barrier, inc=1, device_id={"ctx": lax.rem(c + d, CTX)}, device_id_type=MESH
        )

    def weights(m):
        return (
            pltpu.make_async_copy(wk_ref.at[m], wk.at[m], wkv_sem.at[0, m]),
            pltpu.make_async_copy(wv_ref.at[m], wv.at[m], wkv_sem.at[1, m]),
        )

    route = routes_ref[...]
    member = (iota((MEM * LOCAL, TOK), 0) == route).astype(F32)
    upper_tok = ones_where(iota((TOK, TOK), 0) <= iota((TOK, TOK), 1))
    place = jnp.sum(mm(member.astype(BF16), upper_tok) * member, axis=0, keepdims=True)
    slots = route * CAP + place.astype(jnp.int32) - 1
    totals = jnp.sum(member, axis=1, keepdims=True)
    counts[...] = jnp.zeros_like(counts)
    for to in range(MEM):
        counts[to, 0:LOCAL, :] = jnp.broadcast_to(
            totals[to * LOCAL : (to + 1) * LOCAL], (LOCAL, 128)
        )
    tok_load.wait()

    def x_copy(d, m):
        to = lax.rem(z + d, MEM)
        return pltpu.make_async_remote_copy(
            outgoing.at[m, to], xbuf.at[m, aligned(z, CAP), mine], x_send.at[d, m],
            x_recv.at[d, m], device_id={"mem": to}, device_id_type=MESH,
        )

    def x_arrival(d, m):
        src = lax.rem(z + MEM - d, MEM)
        return pltpu.make_async_remote_copy(
            outgoing.at[m, z], xbuf.at[m, aligned(src, CAP), mine], x_send.at[d, m],
            x_recv.at[d, m], device_id={"mem": src}, device_id_type=MESH,
        )

    def own_copy(m):
        return pltpu.make_async_copy(
            outgoing.at[m, z], xbuf.at[m, aligned(z, CAP), mine], own_sem.at[m]
        )

    def forward(d, m):
        src = lax.rem(z + MEM - d, MEM)
        landed = xbuf.at[m, aligned(src, CAP), mine]
        return pltpu.make_async_remote_copy(
            landed if d else outgoing.at[m, z], landed, f_send.at[d, m], f_recv.at[d, m],
            device_id=other, device_id_type=MESH,
        )

    def forward_arrival(d, m):
        src = lax.rem(z + MEM - d, MEM)
        landed = xbuf.at[m, aligned(src, CAP), aligned(1 - half, DH)]
        return pltpu.make_async_remote_copy(
            landed, landed, f_send.at[d, m], f_recv.at[d, m],
            device_id=other, device_id_type=MESH,
        )

    def count_copy(d):
        to = lax.rem(z + d, MEM)
        return pltpu.make_async_remote_copy(
            counts.at[to], cnt.at[z], c_send.at[d], c_recv.at[d],
            device_id={"mem": to}, device_id_type=MESH,
        )

    def gather(m):
        at = iota((ROWS, TOK), 0)
        slot = (at // CAP * LOCAL + m) * CAP + at % CAP
        rows = mm(ones_where(slot == slots), tok[...]).astype(BF16)
        outgoing[m] = rows.reshape(MEM, CAP, DH)

    def launch(m):
        for d in (2, 1, 3):
            x_copy(d, m).start()
        forward(0, m).start()
        own_copy(m).start()

    gather(0)
    pl.semaphore_wait(barrier, CTX - 1 + MEM)
    for d in range(1, MEM):
        count_copy(d).start()
    launch(0)
    for copy in weights(0):
        copy.start()
    cnt[z] = counts[z]

    @pl.loop(1, LOCAL)
    def _(m):
        gather(m)
        launch(m)
        for copy in weights(m):
            copy.start()

    wq_load = pltpu.make_async_copy(wq_ref, wq, load_sem.at[1])
    wq_load.start()
    wo_load = pltpu.make_async_copy(wo_ref, wo, load_sem.at[2])
    wo_load.start()

    def pass_on(m):
        for d in (1, 3, 2):
            x_arrival(d, m).wait_recv()
            forward(d, m).start()

    pass_on(0)
    for d in range(1, MEM):
        src = lax.rem(z + MEM - d, MEM)
        pltpu.make_async_remote_copy(
            counts.at[z], cnt.at[src], c_send.at[d], c_recv.at[d],
            device_id={"mem": src}, device_id_type=MESH,
        ).wait_recv()

    def map_copy(p):
        return pltpu.make_async_remote_copy(
            mw.at[p], maps.at[c], map_send.at[p], map_recv.at[c],
            device_id={"ctx": p}, device_id_type=MESH,
        )

    def keep_map(p):
        return pltpu.make_async_copy(mw.at[p], maps.at[c], own_sem.at[LOCAL])

    def fade_of(g_col, g_row):
        lower = iota((ROWS, ROWS), 0) >= iota((ROWS, ROWS), 1)
        return jnp.where(lower, jnp.exp(jnp.where(lower, g_col - g_row, 0.0)), 0.0)

    gates[...] = jnp.zeros_like(gates)

    @pl.loop(0, LOCAL)
    def _(m):
        for copy in weights(m):
            copy.wait()
        own_copy(m).wait()
        for d in range(MEM):
            forward_arrival(d, m).wait_recv()
        x = xbuf[m]
        gates[0:HEADS, :] = wb_ref[m]
        gates[HEADS : 2 * HEADS, :] = wd_ref[m]
        logits = mm_nt(gates[...], x)
        keys_all = mm(x, wk[m])
        values_all = mm(x, wv[m])

        lane = iota((1, 128), 1)
        cnt_of = [cnt[src, pl.ds(m, 1), :] for src in range(MEM)]
        cnt_row = jnp.concatenate(
            [
                jnp.where(lane < CAP, cnt_of[0], cnt_of[1]),
                jnp.where(lane < CAP, cnt_of[2], cnt_of[3]),
            ],
            axis=1,
        )
        live = ((iota((1, ROWS), 1) & (CAP - 1)).astype(F32) < cnt_row).astype(F32)
        gate = iota((16, 1), 0)
        rate = jnp.zeros((16, 1), F32)
        for h in heads:
            rate = jnp.where(gate == HEADS + h, rate_ref[m, h], rate)
        strength = jax.nn.sigmoid(logits) * live
        soft = jnp.maximum(logits, 0.0) + jnp.log1p(jnp.exp(-jnp.abs(logits)))
        forget = -rate * soft * live
        row, col = iota((ROWS, ROWS), 0), iota((ROWS, ROWS), 1)
        apart = row ^ col
        upper = ones_where(row <= col)
        hi, mid = split(forget)
        low = (forget - hi.astype(F32) - mid.astype(F32)).astype(BF16)
        total_t = mm(hi, upper) + mm(mid, upper) + mm(low, upper)
        both_t = jnp.where(gate < HEADS, strength, total_t)
        both = jnp.concatenate([both_t, jnp.zeros((112, ROWS), F32)], axis=0).T
        total_ts[m] = both_t
        total_s[m] = both

        mixing = [None] * HEADS
        inverse = [None] * HEADS
        target = [None] * HEADS
        tails = [None] * HEADS
        for h in heads:
            at = slice(h * K, (h + 1) * K)
            k = unit(keys_all[:, at])
            k_hi, k_lo = split(k)
            keys_s[m, h, :, :K] = k_hi
            keys_s[m, h, :, K:] = k_lo
            gram = mm_nt(
                jnp.concatenate([k_hi, k_lo], axis=1), jnp.concatenate([k_hi, k_hi], axis=1)
            ) + mm_nt(k_hi, k_lo)
            g_col = both[:, HEADS + h : HEADS + h + 1]
            beta = both[:, h : h + 1]
            mix = gram * fade_of(g_col, both_t[HEADS + h : HEADS + h + 1, :]) * beta
            mixing[h] = jnp.where(row > col, mix, 0.0)
            target[h] = jnp.concatenate(
                [(beta * jnp.exp(g_col)) * k, beta * values_all[:, at]], axis=1
            )
            tails[h] = k * jnp.exp(g_col[ROWS - 1 : ROWS, :] - g_col)
            inverse[h] = jnp.where(apart == 1, -mixing[h], 0.0).astype(BF16)
        eye = ones_where(row == col)
        mix_hi = [mixing[h].astype(BF16) for h in heads]
        inverse = [inverse[h] + eye for h in heads]
        size = 2
        while size < ROWS // 2:
            if size < 16:
                here = (apart >= size) & (apart < 2 * size)
                mid_way = [
                    jnp.where(here, mm(mix_hi[h], inverse[h]), 0.0).astype(BF16) for h in heads
                ]
                update = [mm(inverse[h], mid_way[h]).astype(BF16) for h in heads]
            else:
                near = level_rows(apart, size)
                here = (near >= size) & (near < 2 * size)
                mid_way = [
                    jnp.where(here, mm(level_rows(mix_hi[h], size), inverse[h]), 0.0).astype(BF16)
                    for h in heads
                ]
                update = [
                    spread_rows(
                        mm(level_rows(inverse[h], size), spread_rows(mid_way[h], size)).astype(
                            BF16
                        ),
                        size,
                    )
                    for h in heads
                ]
            inverse = [inverse[h] - update[h] for h in heads]
            size *= 2
        mid_way = [mm(mix_hi[h][K:, :K], inverse[h][:K, :K]).astype(BF16) for h in heads]
        corner = [mm(inverse[h][K:, K:], mid_way[h]).astype(BF16) for h in heads]
        inverse = [
            jnp.concatenate(
                [
                    inverse[h][:K],
                    jnp.concatenate([-corner[h], inverse[h][K:, K:]], axis=1),
                ],
                axis=0,
            )
            - eye
            for h in heads
        ]
        guess = [target[h] + mm(inverse[h], target[h].astype(BF16)) for h in heads]
        rest = [None] * HEADS
        for h in heads:
            g_hi, g_lo = split(guess[h])
            m_lo = (mixing[h] - mix_hi[h].astype(F32)).astype(BF16)
            applied = mm(mix_hi[h], g_hi) + mm(m_lo, g_hi) + mm(mix_hi[h], g_lo)
            rest[h] = target[h] - guess[h] - applied
        diagonal = iota((K, K), 0) == iota((K, K), 1)
        for h in heads:
            y = guess[h] + rest[h] + mm(inverse[h], rest[h].astype(BF16))
            y_hi, y_lo = split(y)
            solved_hi[m, h] = y_hi
            solved_lo[m, h] = y_lo
            t_hi, t_lo = split(tails[h].T)
            out = mm(t_hi, y_hi) + mm(t_lo, y_hi) + mm(t_hi, y_lo)
            last = jnp.exp(both[ROWS - 1 : ROWS, HEADS + h : HEADS + h + 1])
            p = m * HEADS + h
            mw[p, :, :K] = (jnp.where(diagonal, last, 0.0) - out[:, :K]).astype(BF16)
            mw[p, :, K:] = out[:, K:].astype(BF16)
        for h in heads:
            p = m * HEADS + h

            @pl.when((p != c) & (c < CTX - 1))
            def _():
                map_copy(p).start()

            @pl.when(p == c)
            def _():
                keep_map(p).start()

        @pl.when(m + 1 < LOCAL)
        def _():
            pass_on(m + 1)

    w_copy = pltpu.make_async_remote_copy(
        wo_ref, w_other, pair_send.at[0], pair_recv.at[0], device_id=other, device_id_type=MESH
    )
    w_copy.start()
    wq_load.wait()

    def local_output(m):
        query_all = mm(xbuf[m], wq[...])
        both = total_s[m]
        for h in heads:
            q = unit(query_all[:, h * K : (h + 1) * K])
            q_hi, q_lo = split(q)
            k_hi, k_lo = keys_s[m, h, :, :K], keys_s[m, h, :, K:]
            gram = mm_nt(
                jnp.concatenate([q_hi, q_lo], axis=1), jnp.concatenate([k_hi, k_hi], axis=1)
            ) + mm_nt(q_hi, k_lo)
            g_col = both[:, HEADS + h : HEADS + h + 1]
            g_row = total_ts[m, HEADS + h : HEADS + h + 1, :]
            s_hi, s_lo = split(gram * fade_of(g_col, g_row))
            y_hi, y_lo = solved_hi[m, h], solved_lo[m, h]
            out = mm(s_hi, y_hi) + mm(s_lo, y_hi) + mm(s_hi, y_lo)
            base[m, :, h * K : (h + 1) * K] = out[:, K:]
            r_hi, r_lo = split(q * jnp.exp(g_col) - out[:, :K])
            reach[m, :, 2 * h * K : (2 * h + 1) * K] = r_hi
            reach[m, :, (2 * h + 1) * K : (2 * h + 2) * K] = r_lo

    @pl.loop(0, LOCAL // 2)
    def _(m):
        local_output(m)

    def state_copy(to):
        return pltpu.make_async_remote_copy(
            states.at[to], entering.at[c], state_send.at[to], state_recv.at[c],
            device_id={"ctx": to}, device_id_type=MESH,
        )

    keep_map(c).wait()
    state = None
    for j in range(CTX - 1):

        @pl.when(c != j)
        def _():
            pltpu.make_async_remote_copy(
                mw.at[j], maps.at[j], map_send.at[j], map_recv.at[j],
                device_id={"ctx": j}, device_id_type=MESH,
            ).wait_recv()

        add = maps[j, :, K:].astype(F32)
        if j == 0:
            state = add
        else:
            step = maps[j, :, :K]
            s_hi, s_lo = split(state)
            state = add + mm(
                jnp.concatenate([step, step], axis=1), jnp.concatenate([s_hi, s_lo], axis=0)
            )
        states[j + 1] = state.astype(BF16)

        @pl.when(c != j + 1)
        def _():
            state_copy(j + 1).start()

    @pl.loop(LOCAL // 2, LOCAL)
    def _(m):
        local_output(m)

    def ret_copy(d, m):
        to = lax.rem(z + d, MEM)
        return pltpu.make_async_remote_copy(
            reply.at[m, to], returned.at[z, m], ret_send.at[d, m], ret_recv.at[d, m],
            device_id={"mem": to}, device_id_type=MESH,
        )

    keep_state = pltpu.make_async_copy(states.at[c], entering.at[c], own_sem.at[LOCAL])

    @pl.when(c == 0)
    def _():
        entering[...] = jnp.zeros_like(entering)

    @pl.when(c > 0)
    def _():
        keep_state.start()
        keep_state.wait()

    @pl.loop(0, LOCAL)
    def _(m):
        for h in heads:
            p = m * HEADS + h

            @pl.when((c > 0) & (p != c))
            def _():
                pltpu.make_async_remote_copy(
                    states.at[1], entering.at[p], state_send.at[1], state_recv.at[p],
                    device_id={"ctx": p}, device_id_type=MESH,
                ).wait_recv()

        for h in heads:
            at = slice(h * K, (h + 1) * K)
            s = entering[m * HEADS + h]
            heads_out = base[m, :, at] + mm(
                reach[m, :, 2 * h * K : (2 * h + 2) * K], jnp.concatenate([s, s], axis=0)
            )
            scale = lax.rsqrt(jnp.mean(heads_out * heads_out, axis=1, keepdims=True) + 1e-05)
            normed = (heads_out * scale * gain_ref[:, at]).astype(BF16)
            reply[m, :, :, at] = normed.reshape(MEM, CAP, K)
        for d in (2, 1, 3):
            ret_copy(d, m).start()

    column = jnp.broadcast_to(slots.astype(F32), (128, TOK)).T[:, 0:1].astype(jnp.int32)

    def pick(src, rows):
        chosen = ones_where(iota((TOK, ROWS), 1) + src * ROWS == column)
        return mm(chosen, rows)

    own_rows = jnp.concatenate([reply[m, z] for m in range(LOCAL)], axis=0)
    total = pick(z, own_rows)
    for d in (1, 3, 2):
        src = lax.rem(z + MEM - d, MEM)
        for m in range(LOCAL):
            pltpu.make_async_remote_copy(
                reply.at[m, z], returned.at[src, m], ret_send.at[d, m], ret_recv.at[d, m],
                device_id={"mem": src}, device_id_type=MESH,
            ).wait_recv()
        total = total + pick(src, returned[src].reshape(ROWS, WIDTH))
    picked[...] = total.astype(BF16)
    swap = pltpu.make_async_remote_copy(
        picked.at[aligned(1 - half, TOK // 2)], partner, pair_send.at[1], pair_recv.at[1],
        device_id=other, device_id_type=MESH,
    )
    swap.start()
    wo_load.wait()
    mixed = mm(picked[aligned(half, TOK // 2), :], wo[...])
    w_copy.wait()
    swap.wait()
    out_ref[...] = (mixed + mm(partner[...], w_other[...])).astype(BF16)

    for d in range(1, MEM):
        count_copy(d).wait_send()

    @pl.loop(0, LOCAL)
    def _(m):
        for d in range(1, MEM):
            x_copy(d, m).wait_send()
            ret_copy(d, m).wait_send()
        for d in range(MEM):
            forward(d, m).wait_send()
        for h in heads:
            p = m * HEADS + h

            @pl.when((p != c) & (c < CTX - 1))
            def _():
                map_copy(p).wait_send()

    @pl.loop(1, CTX)
    def _(j):
        @pl.when(c != j)
        def _():
            state_copy(j).wait_send()


def per_device(
    tokens, routes, w_query, w_key, w_value, w_beta, w_decay, decay_rate, norm_gain, w_out
):
    dma = pltpu.SemaphoreType.DMA
    vmem = pltpu.VMEM
    in_vmem = pl.BlockSpec(memory_space=pltpu.VMEM)
    in_place = pl.BlockSpec(memory_space=pl.ANY)
    return pl.pallas_call(
        layer_kernel,
        name="layer",
        out_shape=jax.ShapeDtypeStruct((TOK // 2, D), BF16),
        in_specs=[
            pl.BlockSpec(memory_space=pltpu.SMEM), in_vmem, in_place, in_place, in_place,
            in_place, in_vmem, in_vmem, in_vmem, in_place,
        ],
        out_specs=in_vmem,
        scratch_shapes=[
            vmem((TOK, DH), BF16),
            vmem((LOCAL, MEM, CAP, DH), BF16),
            vmem((MEM, 8, 128), F32),
            vmem((MEM, 8, 128), F32),
            vmem((LOCAL, ROWS, D), BF16),
            vmem((D, WIDTH), BF16),
            vmem((LOCAL, D, WIDTH), BF16),
            vmem((LOCAL, D, WIDTH), BF16),
            vmem((16, D), BF16),
            vmem((LOCAL, ROWS, 128), F32),
            vmem((LOCAL, 16, ROWS), F32),
            vmem((LOCAL, HEADS, ROWS, 2 * K), BF16),
            vmem((LOCAL, HEADS, ROWS, 2 * K), BF16),
            vmem((LOCAL, HEADS, ROWS, 2 * K), BF16),
            vmem((CTX, K, 2 * K), BF16),
            vmem((CTX, K, 2 * K), BF16),
            vmem((CTX, K, K), BF16),
            vmem((CTX, K, K), BF16),
            vmem((LOCAL, ROWS, WIDTH), F32),
            vmem((LOCAL, ROWS, 2 * WIDTH), BF16),
            vmem((LOCAL, MEM, CAP, WIDTH), BF16),
            vmem((MEM, LOCAL, CAP, WIDTH), BF16),
            vmem((TOK, WIDTH), BF16),
            vmem((TOK // 2, WIDTH), BF16),
            vmem((WIDTH, D), BF16),
            vmem((WIDTH, D), BF16),
            dma((3,)), dma((2, LOCAL)), dma((LOCAL + 1,)),
            dma((MEM, LOCAL)), dma((MEM, LOCAL)), dma((MEM,)), dma((MEM,)),
            dma((MEM, LOCAL)), dma((MEM, LOCAL)),
            dma((CTX,)), dma((CTX,)), dma((CTX,)), dma((CTX,)),
            dma((MEM, LOCAL)), dma((MEM, LOCAL)), dma((2,)), dma((2,)),
        ],
        compiler_params=pltpu.CompilerParams(
            collective_id=0, has_side_effects=True, vmem_limit_bytes=67_043_328
        ),
    )(
        decay_rate,
        routes.reshape(1, TOK),
        tokens,
        w_query,
        w_key,
        w_value,
        jnp.swapaxes(w_beta, 1, 2),
        jnp.swapaxes(w_decay, 1, 2),
        norm_gain.reshape(1, WIDTH),
        w_out,
    )


def solution(mesh):
    in_specs = (
        P(("ctx", "mem"), None),
        P(("ctx", "mem"), None),
        P(None, "half"),
        P("mem", None, "half"),
        P("mem", None, "half"),
        P("mem", None, "half"),
        P("mem", None, "half"),
        P("mem", "half"),
        P("half"),
        P("half", None),
    )
    out_specs = P(("ctx", "mem", "half"), None)
    return jax.shard_map(
        per_device, mesh=mesh, in_specs=in_specs, out_specs=out_specs, check_vma=False
    )
```

time: 685 us -> 92.3 us (0.13); the launches traced: 675 us -> 91.5 us
  waiting for transfers between devices: 358 us -> 0 us
  matrix products: 195 us -> 0 us
  Pallas kernels: 0 us -> 89.2 us
  local copies, waits for them, and re-layouts: 53 us -> 2.3 us
  starting transfers between devices: 43.6 us -> 0 us
  between operations: 14.3 us -> 0.01 us
  other arithmetic: 10.5 us -> 0 us
    ppermute x15 -> x0, waiting for transfers between devices: 301 us -> none  [shifted(): return lax.ppermute(shard, axis, pairs)]
    dot_general x55 -> x0, matrix products: 195 us -> none  [the longest x15 55.9 us: forward_state_update(): jnp.einsum('bkl,blv->bkv', whole_map, incoming, precision=precise_result)]
    pallas_call x0 -> x1, Pallas kernels: none -> 89.2 us  [per_device(): pl.pallas_call(layer_kernel, name='layer', out_shape=jax.ShapeDtypeStruct...]
    ppermute x15 -> x0, starting transfers between devices: 29.8 us -> none  [shifted(): return lax.ppermute(shard, axis, pairs)]
    reshape x4 -> x0, local copies, waits for them, and re-layouts: 29.2 us -> none  [the longest x1 12.5 us: per_device(): w_value.reshape(mem_local, width, heads_here, value_size)]
    reduce_scatter x1 -> x0, waiting for transfers between devices: 28.5 us -> none  [per_device(): lax.psum_scatter(jnp.dot(picked, w_out, preferred_element_type=jnp.float3...]
    all_to_all x3 -> x0, waiting for transfers between devices: 28 us -> none  [the longest x1 18.4 us: per_device(): lax.all_to_all(outgoing, 'mem', split_axis=0, concat_axis=0, tiled=True)]
    all_to_all x3 -> x0, starting transfers between devices: 13.7 us -> none  [the longest x1 5.21 us: per_device(): lax.all_to_all(outgoing, 'mem', split_axis=0, concat_axis=0, tiled=True)]
  transfers between devices with their start and end apart: 19 -> 0, of which waited for: 18 -> 0; matrix products, arithmetic and copies ran while one was open for 5% -> 0% of each run, Pallas kernels for 0% -> 0%
where the time goes in v2:
time: 92.3 us; the launch traced here: 91.5 us
  Pallas kernels  89.2 us (97%)
  local copies, waits for them, and re-layouts  2.3 us (2%)
    pallas_call x1, Pallas kernels, per_device(): pl.pallas_call(layer_kernel, name='layer', out_shape=jax.ShapeDtypeStruct...  89.2 us
    unnamed x1, local copies, waits for them, and re-layouts  2.3 us

profile of v2, /device:TPU:25, one launch (start us, length us, event | category | flops | bytes accessed | tf_op | source)
XLA Modules:
  0.0 91.5 jit_solution(11908502890771224530)
XLA Ops:
  0.0 89.2 %layer.1 = bf16[256,2048]{1,0:T(8,128)(2,1)} custom-call(f32[4,4]{1,0:T(4,128)} %rate_ref.1, s32[1,512]{1,0:T(1,128)} %bitcast.6, bf16[512,2048]{1,0:T(8,128)(2,1)} %tok_ref.1, bf16[2048,512]{1,0:T(8,128)(2,1)} %wq_ref.1, bf16[4,2048,512]{2,1,0:T(8,128)(2,1)} %wk_ref.1, bf16[4,2048,512]{2,1,0:T(8,128)(2,1)} %wv_ref.1, bf16[4,4,2048]{2,1,0:T(4,128)(2,1)} %bitcast.4, ...), custom_call_target="tpu_custom_call" | custom-call | tf_op jit(solution)/shard_map/layer/pallas_call | solution.py:524
  89.2 2.3 %copy.12 = bf16[256,2048]{1,0:T(8,128)(2,1)} copy(bf16[256,2048]{1,0:T(8,128)(2,1)} %layer.1) | data formatting | bytes 2097152

commit v3 on v2

--- a/solution.py
+++ b/solution.py
@@ -51,16 +51,49 @@
 
 def level_rows(x, size):
     return jnp.concatenate(
-        [x[at + size : at + 2 * size] for at in range(0, ROWS, 2 * size)], axis=0
+        [x[at + size : at + 2 * size] for at in range(0, x.shape[0], 2 * size)], axis=0
     )
 
 
 def spread_rows(x, size):
     gap = jnp.zeros((size, x.shape[1]), x.dtype)
     parts = []
-    for at in range(0, ROWS // 2, size):
+    for at in range(0, x.shape[0], size):
         parts += [gap, x[at : at + size]]
     return jnp.concatenate(parts, axis=0)
+
+
+def unit_lower_inverses(blocks):
+    side = blocks[0].shape[0]
+    row, col = iota((side, side), 0), iota((side, side), 1)
+    apart = row ^ col
+    eye = ones_where(row == col)
+    low = [b.astype(BF16) for b in blocks]
+    inverse = [jnp.where(apart == 1, -b, 0.0).astype(BF16) + eye for b in blocks]
+    size = 2
+    while size < side:
+        whole = size < 16
+        pick = (lambda x: x) if whole else (lambda x: level_rows(x, size))
+        put = (lambda x: x) if whole else (lambda x: spread_rows(x, size))
+        near = pick(apart)
+        here = (near >= size) & (near < 2 * size)
+        mid_way = [
+            jnp.where(here, mm(pick(a), x), 0.0).astype(BF16) for a, x in zip(low, inverse)
+        ]
+        update = [
+            put(mm(pick(x), put(y)).astype(BF16)) for x, y in zip(inverse, mid_way)
+        ]
+        inverse = [x - u for x, u in zip(inverse, update)]
+        size *= 2
+    return inverse, eye
+
+
+def three_pass(a, b):
+    a_hi, a_lo = a
+    b_hi, b_lo = b
+    return mm(
+        jnp.concatenate([a_hi, a_lo, a_hi], axis=1), jnp.concatenate([b_hi, b_hi, b_lo], axis=0)
+    )
 
 
 def layer_kernel(
@@ -78,6 +111,11 @@
     other = {"half": 1 - half}
     mine = aligned(half, DH)
     heads = range(HEADS)
+    own_stage = lax.rem(c // 4 + 2 * half, LOCAL)
+    own_pair = own_stage * HEADS + lax.rem(c, 4)
+
+    def owner(m, h):
+        return lax.rem(m + 2 * half, LOCAL) * 4 + h
 
     tok_load = pltpu.make_async_copy(tok_ref.at[:, mine], tok, load_sem.at[0])
     tok_load.start()
@@ -199,14 +237,12 @@
             device_id={"mem": src}, device_id_type=MESH,
         ).wait_recv()
 
-    def map_copy(p):
+    def map_copy(m, h):
+        p = m * HEADS + h
         return pltpu.make_async_remote_copy(
             mw.at[p], maps.at[c], map_send.at[p], map_recv.at[c],
-            device_id={"ctx": p}, device_id_type=MESH,
-        )
-
-    def keep_map(p):
-        return pltpu.make_async_copy(mw.at[p], maps.at[c], own_sem.at[LOCAL])
+            device_id={"ctx": owner(m, h)}, device_id_type=MESH,
+        )
 
     def fade_of(g_col, g_row):
         lower = iota((ROWS, ROWS), 0) >= iota((ROWS, ROWS), 1)
@@ -245,9 +281,7 @@
         strength = jax.nn.sigmoid(logits) * live
         soft = jnp.maximum(logits, 0.0) + jnp.log1p(jnp.exp(-jnp.abs(logits)))
         forget = -rate * soft * live
-        row, col = iota((ROWS, ROWS), 0), iota((ROWS, ROWS), 1)
-        apart = row ^ col
-        upper = ones_where(row <= col)
+        upper = ones_where(iota((ROWS, ROWS), 0) <= iota((ROWS, ROWS), 1))
         hi, mid = split(forget)
         low = (forget - hi.astype(F32) - mid.astype(F32)).astype(BF16)
         total_t = mm(hi, upper) + mm(mid, upper) + mm(low, upper)
@@ -256,13 +290,15 @@
         total_ts[m] = both_t
         total_s[m] = both
 
-        mixing = [None] * HEADS
-        inverse = [None] * HEADS
-        target = [None] * HEADS
-        tails = [None] * HEADS
+        keys, corner, target = [None] * HEADS, [None] * HEADS, [None] * HEADS
+        blocks = [None] * (2 * HEADS)
+        last = both[ROWS - 1 : ROWS, :]
+        square = iota((K, K), 0), iota((K, K), 1)
+        strict = square[0] > square[1]
         for h in heads:
             at = slice(h * K, (h + 1) * K)
             k = unit(keys_all[:, at])
+            keys[h] = k
             k_hi, k_lo = split(k)
             keys_s[m, h, :, :K] = k_hi
             keys_s[m, h, :, K:] = k_lo
@@ -270,85 +306,66 @@
                 jnp.concatenate([k_hi, k_lo], axis=1), jnp.concatenate([k_hi, k_hi], axis=1)
             ) + mm_nt(k_hi, k_lo)
             g_col = both[:, HEADS + h : HEADS + h + 1]
+            g_row = both_t[HEADS + h : HEADS + h + 1, :]
             beta = both[:, h : h + 1]
-            mix = gram * fade_of(g_col, both_t[HEADS + h : HEADS + h + 1, :]) * beta
-            mixing[h] = jnp.where(row > col, mix, 0.0)
+            for b in range(2):
+                part = slice(b * K, (b + 1) * K)
+                gap = jnp.minimum(g_col[part] - g_row[:, part], 0.0)
+                mix = gram[part, part] * jnp.exp(gap) * beta[part]
+                blocks[2 * h + b] = jnp.where(strict, mix, 0.0)
+            corner[h] = gram[K:, :K] * jnp.exp(g_col[K:] - g_row[:, :K]) * beta[K:]
             target[h] = jnp.concatenate(
                 [(beta * jnp.exp(g_col)) * k, beta * values_all[:, at]], axis=1
             )
-            tails[h] = k * jnp.exp(g_col[ROWS - 1 : ROWS, :] - g_col)
-            inverse[h] = jnp.where(apart == 1, -mixing[h], 0.0).astype(BF16)
-        eye = ones_where(row == col)
-        mix_hi = [mixing[h].astype(BF16) for h in heads]
-        inverse = [inverse[h] + eye for h in heads]
-        size = 2
-        while size < ROWS // 2:
-            if size < 16:
-                here = (apart >= size) & (apart < 2 * size)
-                mid_way = [
-                    jnp.where(here, mm(mix_hi[h], inverse[h]), 0.0).astype(BF16) for h in heads
-                ]
-                update = [mm(inverse[h], mid_way[h]).astype(BF16) for h in heads]
-            else:
-                near = level_rows(apart, size)
-                here = (near >= size) & (near < 2 * size)
-                mid_way = [
-                    jnp.where(here, mm(level_rows(mix_hi[h], size), inverse[h]), 0.0).astype(BF16)
-                    for h in heads
-                ]
-                update = [
-                    spread_rows(
-                        mm(level_rows(inverse[h], size), spread_rows(mid_way[h], size)).astype(
-                            BF16
-                        ),
-                        size,
-                    )
-                    for h in heads
-                ]
-            inverse = [inverse[h] - update[h] for h in heads]
-            size *= 2
-        mid_way = [mm(mix_hi[h][K:, :K], inverse[h][:K, :K]).astype(BF16) for h in heads]
-        corner = [mm(inverse[h][K:, K:], mid_way[h]).astype(BF16) for h in heads]
+        inverse, eye = unit_lower_inverses(blocks)
+        none = jnp.zeros((K, K), BF16)
+        cross = [
+            mm(corner[h].astype(BF16), inverse[2 * h]).astype(BF16) for h in heads
+        ]
+        cross = [mm(inverse[2 * h + 1], cross[h]).astype(BF16) for h in heads]
         inverse = [
             jnp.concatenate(
                 [
-                    inverse[h][:K],
-                    jnp.concatenate([-corner[h], inverse[h][K:, K:]], axis=1),
+                    jnp.concatenate([inverse[2 * h] - eye, none], axis=1),
+                    jnp.concatenate([-cross[h], inverse[2 * h + 1] - eye], axis=1),
                 ],
                 axis=0,
             )
-            - eye
             for h in heads
         ]
         guess = [target[h] + mm(inverse[h], target[h].astype(BF16)) for h in heads]
         rest = [None] * HEADS
         for h in heads:
-            g_hi, g_lo = split(guess[h])
-            m_lo = (mixing[h] - mix_hi[h].astype(F32)).astype(BF16)
-            applied = mm(mix_hi[h], g_hi) + mm(m_lo, g_hi) + mm(mix_hi[h], g_lo)
-            rest[h] = target[h] - guess[h] - applied
-        diagonal = iota((K, K), 0) == iota((K, K), 1)
-        for h in heads:
-            y = guess[h] + rest[h] + mm(inverse[h], rest[h].astype(BF16))
-            y_hi, y_lo = split(y)
-            solved_hi[m, h] = y_hi
-            solved_lo[m, h] = y_lo
-            t_hi, t_lo = split(tails[h].T)
-            out = mm(t_hi, y_hi) + mm(t_lo, y_hi) + mm(t_hi, y_lo)
-            last = jnp.exp(both[ROWS - 1 : ROWS, HEADS + h : HEADS + h + 1])
+            a_hi, a_lo = split(blocks[2 * h])
+            b_hi, b_lo = split(blocks[2 * h + 1])
+            c_hi, c_lo = split(corner[h])
+            mix_hi = jnp.concatenate(
+                [jnp.concatenate([a_hi, none], axis=1), jnp.concatenate([c_hi, b_hi], axis=1)],
+                axis=0,
+            )
+            mix_lo = jnp.concatenate(
+                [jnp.concatenate([a_lo, none], axis=1), jnp.concatenate([c_lo, b_lo], axis=1)],
+                axis=0,
+            )
+            rest[h] = target[h] - guess[h] - three_pass((mix_hi, mix_lo), split(guess[h]))
+        solved = [
+            guess[h] + rest[h] + mm(inverse[h], rest[h].astype(BF16)) for h in heads
+        ]
+        diagonal = square[0] == square[1]
+        for h in heads:
+            y = split(solved[h])
+            solved_hi[m, h], solved_lo[m, h] = y
+            g_last = last[:, HEADS + h : HEADS + h + 1]
+            tail = keys[h] * jnp.exp(g_last - both[:, HEADS + h : HEADS + h + 1])
+            out = three_pass(split(tail.T), y)
             p = m * HEADS + h
-            mw[p, :, :K] = (jnp.where(diagonal, last, 0.0) - out[:, :K]).astype(BF16)
+            mw[p, :, :K] = (jnp.where(diagonal, jnp.exp(g_last), 0.0) - out[:, :K]).astype(BF16)
             mw[p, :, K:] = out[:, K:].astype(BF16)
         for h in heads:
-            p = m * HEADS + h
-
-            @pl.when((p != c) & (c < CTX - 1))
+
+            @pl.when((m * HEADS + h != own_pair) & (c < CTX - 1))
             def _():
-                map_copy(p).start()
-
-            @pl.when(p == c)
-            def _():
-                keep_map(p).start()
+                map_copy(m, h).start()
 
         @pl.when(m + 1 < LOCAL)
         def _():
@@ -372,53 +389,49 @@
             ) + mm_nt(q_hi, k_lo)
             g_col = both[:, HEADS + h : HEADS + h + 1]
             g_row = total_ts[m, HEADS + h : HEADS + h + 1, :]
-            s_hi, s_lo = split(gram * fade_of(g_col, g_row))
-            y_hi, y_lo = solved_hi[m, h], solved_lo[m, h]
-            out = mm(s_hi, y_hi) + mm(s_lo, y_hi) + mm(s_hi, y_lo)
+            scores = split(gram * fade_of(g_col, g_row))
+            out = three_pass(scores, (solved_hi[m, h], solved_lo[m, h]))
             base[m, :, h * K : (h + 1) * K] = out[:, K:]
             r_hi, r_lo = split(q * jnp.exp(g_col) - out[:, :K])
             reach[m, :, 2 * h * K : (2 * h + 1) * K] = r_hi
             reach[m, :, (2 * h + 1) * K : (2 * h + 2) * K] = r_lo
 
-    @pl.loop(0, LOCAL // 2)
-    def _(m):
-        local_output(m)
-
     def state_copy(to):
         return pltpu.make_async_remote_copy(
-            states.at[to], entering.at[c], state_send.at[to], state_recv.at[c],
+            states.at[to], entering.at[own_pair], state_send.at[to], state_recv.at[own_pair],
             device_id={"ctx": to}, device_id_type=MESH,
         )
 
-    keep_map(c).wait()
-    state = None
-    for j in range(CTX - 1):
-
-        @pl.when(c != j)
-        def _():
-            pltpu.make_async_remote_copy(
-                mw.at[j], maps.at[j], map_send.at[j], map_recv.at[j],
-                device_id={"ctx": j}, device_id_type=MESH,
-            ).wait_recv()
-
-        add = maps[j, :, K:].astype(F32)
-        if j == 0:
-            state = add
-        else:
-            step = maps[j, :, :K]
-            s_hi, s_lo = split(state)
-            state = add + mm(
-                jnp.concatenate([step, step], axis=1), jnp.concatenate([s_hi, s_lo], axis=0)
-            )
-        states[j + 1] = state.astype(BF16)
-
-        @pl.when(c != j + 1)
-        def _():
-            state_copy(j + 1).start()
-
-    @pl.loop(LOCAL // 2, LOCAL)
-    def _(m):
-        local_output(m)
+    def run_pair():
+        maps[c] = mw[own_pair]
+        state = None
+        for j in range(CTX - 1):
+
+            @pl.when(c != j)
+            def _():
+                pltpu.make_async_remote_copy(
+                    mw.at[j], maps.at[j], map_send.at[j], map_recv.at[j],
+                    device_id={"ctx": j}, device_id_type=MESH,
+                ).wait_recv()
+
+            add = maps[j, :, K:].astype(F32)
+            if j == 0:
+                state = add
+            else:
+                step = maps[j, :, :K]
+                s_hi, s_lo = split(state)
+                state = add + mm(
+                    jnp.concatenate([step, step], axis=1), jnp.concatenate([s_hi, s_lo], axis=0)
+                )
+            states[j + 1] = state.astype(BF16)
+
+            @pl.when(c != j + 1)
+            def _():
+                state_copy(j + 1).start()
+
+            @pl.when(c == j + 1)
+            def _():
+                entering[own_pair] = states[j + 1]
 
     def ret_copy(d, m):
         to = lax.rem(z + d, MEM)
@@ -427,27 +440,15 @@
             device_id={"mem": to}, device_id_type=MESH,
         )
 
-    keep_state = pltpu.make_async_copy(states.at[c], entering.at[c], own_sem.at[LOCAL])
-
-    @pl.when(c == 0)
-    def _():
-        entering[...] = jnp.zeros_like(entering)
-
-    @pl.when(c > 0)
-    def _():
-        keep_state.start()
-        keep_state.wait()
-
-    @pl.loop(0, LOCAL)
-    def _(m):
+    def send_outputs(m):
         for h in heads:
             p = m * HEADS + h
 
-            @pl.when((c > 0) & (p != c))
+            @pl.when((c > 0) & (p != own_pair))
             def _():
                 pltpu.make_async_remote_copy(
                     states.at[1], entering.at[p], state_send.at[1], state_recv.at[p],
-                    device_id={"ctx": p}, device_id_type=MESH,
+                    device_id={"ctx": owner(m, h)}, device_id_type=MESH,
                 ).wait_recv()
 
         for h in heads:
@@ -461,6 +462,26 @@
             reply[m, :, :, at] = normed.reshape(MEM, CAP, K)
         for d in (2, 1, 3):
             ret_copy(d, m).start()
+
+    @pl.when(c == 0)
+    def _():
+        entering[...] = jnp.zeros_like(entering)
+
+    turn = jnp.where(own_stage < 2, 0, jnp.where(own_stage == 2, 1, 3))
+
+    @pl.loop(0, LOCAL)
+    def _(m):
+        @pl.when(m == turn)
+        def _():
+            run_pair()
+
+        local_output(m)
+
+        @pl.when(m > 0)
+        def _():
+            send_outputs(m - 1)
+
+    send_outputs(LOCAL - 1)
 
     column = jnp.broadcast_to(slots.astype(F32), (128, TOK)).T[:, 0:1].astype(jnp.int32)
 
@@ -501,11 +522,10 @@
         for d in range(MEM):
             forward(d, m).wait_send()
         for h in heads:
-            p = m * HEADS + h
-
-            @pl.when((p != c) & (c < CTX - 1))
+
+            @pl.when((m * HEADS + h != own_pair) & (c < CTX - 1))
             def _():
-                map_copy(p).wait_send()
+                map_copy(m, h).wait_send()
 
     @pl.loop(1, CTX)
     def _(j):
@@ -557,7 +577,7 @@
             vmem((TOK // 2, WIDTH), BF16),
             vmem((WIDTH, D), BF16),
             vmem((WIDTH, D), BF16),
-            dma((3,)), dma((2, LOCAL)), dma((LOCAL + 1,)),
+            dma((3,)), dma((2, LOCAL)), dma((LOCAL,)),
             dma((MEM, LOCAL)), dma((MEM, LOCAL)), dma((MEM,)), dma((MEM,)),
             dma((MEM, LOCAL)), dma((MEM, LOCAL)),
             dma((CTX,)), dma((CTX,)), dma((CTX,)), dma((CTX,)),

time: 92.3 us -> 78.4 us (0.85)
  Pallas kernels: 89.2 us -> 74.6 us
    pallas_call x1, Pallas kernels: 89.2 us -> 74.6 us  [per_device(): pl.pallas_call(layer_kernel, name='layer', out_shape=jax.ShapeDtypeStruct...]
where the time goes in v3:
time: 78.4 us; the launch traced here: 76.9 us
  Pallas kernels  74.6 us (95%)
  local copies, waits for them, and re-layouts  2.3 us (3%)
    pallas_call x1, Pallas kernels, per_device(): pl.pallas_call(layer_kernel, name='layer', out_shape=jax.ShapeDtypeStruct...  74.6 us
    unnamed x1, local copies, waits for them, and re-layouts  2.3 us

profile of v3, /device:TPU:25, one launch (start us, length us, event | category | flops | bytes accessed | tf_op | source)
XLA Modules:
  0.0 76.9 jit_solution(1963608981409955565)
XLA Ops:
  0.0 74.6 %layer.1 = bf16[256,2048]{1,0:T(8,128)(2,1)} custom-call(f32[4,4]{1,0:T(4,128)} %rate_ref.1, s32[1,512]{1,0:T(1,128)} %bitcast.6, bf16[512,2048]{1,0:T(8,128)(2,1)} %tok_ref.1, bf16[2048,512]{1,0:T(8,128)(2,1)} %wq_ref.1, bf16[4,2048,512]{2,1,0:T(8,128)(2,1)} %wk_ref.1, bf16[4,2048,512]{2,1,0:T(8,128)(2,1)} %wv_ref.1, bf16[4,4,2048]{2,1,0:T(4,128)(2,1)} %bitcast.4, ...), custom_call_target="tpu_custom_call" | custom-call | tf_op jit(solution)/shard_map/layer/pallas_call | solution.py:544
  74.6 2.3 %copy.12 = bf16[256,2048]{1,0:T(8,128)(2,1)} copy(bf16[256,2048]{1,0:T(8,128)(2,1)} %layer.1) | data formatting | bytes 2097152

commit v4 on v3

--- a/solution.py
+++ b/solution.py
@@ -63,7 +63,8 @@
     return jnp.concatenate(parts, axis=0)
 
 
-def unit_lower_inverses(blocks):
+def unit_lower_inverses(blocks, beside):
+    beside = list(beside)
     side = blocks[0].shape[0]
     row, col = iota((side, side), 0), iota((side, side), 1)
     apart = row ^ col
@@ -80,11 +81,15 @@
         mid_way = [
             jnp.where(here, mm(pick(a), x), 0.0).astype(BF16) for a, x in zip(low, inverse)
         ]
+        if beside:
+            beside.pop(0)()
         update = [
             put(mm(pick(x), put(y)).astype(BF16)) for x, y in zip(inverse, mid_way)
         ]
         inverse = [x - u for x, u in zip(inverse, update)]
         size *= 2
+    for work in beside:
+        work()
     return inverse, eye
 
 
@@ -99,7 +104,7 @@
 def layer_kernel(
     rate_ref, routes_ref, tok_ref, wq_ref, wk_ref, wv_ref, wb_ref, wd_ref, gain_ref, wo_ref,
     out_ref,
-    tok, outgoing, counts, cnt, xbuf, wq, wk, wv, gates, total_s, total_ts, keys_s, solved_hi,
+    tok, outgoing, counts, cnt, xbuf, wq, wk, wv, gates, kv, logits_s, total_s, total_ts, keys_s, solved_hi,
     solved_lo, mw, maps, states, entering, base, reach, reply, returned, picked, partner, wo,
     w_other,
     load_sem, wkv_sem, own_sem, x_send, x_recv, c_send, c_recv, f_send, f_recv,
@@ -250,19 +255,35 @@
 
     gates[...] = jnp.zeros_like(gates)
 
-    @pl.loop(0, LOCAL)
-    def _(m):
+    def wait_tokens(m):
         for copy in weights(m):
             copy.wait()
         own_copy(m).wait()
         for d in range(MEM):
             forward_arrival(d, m).wait_recv()
-        x = xbuf[m]
-        gates[0:HEADS, :] = wb_ref[m]
-        gates[HEADS : 2 * HEADS, :] = wd_ref[m]
-        logits = mm_nt(gates[...], x)
-        keys_all = mm(x, wk[m])
-        values_all = mm(x, wv[m])
+
+    def projections(m):
+        def gate_part():
+            gates[0:HEADS, :] = wb_ref[m]
+            gates[HEADS : 2 * HEADS, :] = wd_ref[m]
+            logits_s[...] = mm_nt(gates[...], xbuf[m])
+
+        def part(w, at, to):
+            def run():
+                kv[:, to : to + 2 * K] = mm(xbuf[m], w[m, :, at : at + 2 * K])
+
+            return run
+
+        return [gate_part] + [
+            part(w, at, first + at) for w, first in ((wk, 0), (wv, WIDTH)) for at in (0, 2 * K)
+        ]
+
+    def make_maps(m, following):
+        if following is not None:
+            pass_on(following)
+        logits = logits_s[...]
+        keys_all = kv[:, :WIDTH]
+        values_all = kv[:, WIDTH:]
 
         lane = iota((1, 128), 1)
         cnt_of = [cnt[src, pl.ds(m, 1), :] for src in range(MEM)]
@@ -317,7 +338,11 @@
             target[h] = jnp.concatenate(
                 [(beta * jnp.exp(g_col)) * k, beta * values_all[:, at]], axis=1
             )
-        inverse, eye = unit_lower_inverses(blocks)
+        beside = []
+        if following is not None:
+            wait_tokens(following)
+            beside = projections(following)
+        inverse, eye = unit_lower_inverses(blocks, beside)
         none = jnp.zeros((K, K), BF16)
         cross = [
             mm(corner[h].astype(BF16), inverse[2 * h]).astype(BF16) for h in heads
@@ -367,9 +392,15 @@
             def _():
                 map_copy(m, h).start()
 
-        @pl.when(m + 1 < LOCAL)
-        def _():
-            pass_on(m + 1)
+    wait_tokens(0)
+    for work in projections(0):
+        work()
+
+    @pl.loop(0, LOCAL - 1)
+    def _(m):
+        make_maps(m, m + 1)
+
+    make_maps(LOCAL - 1, None)
 
     w_copy = pltpu.make_async_remote_copy(
         wo_ref, w_other, pair_send.at[0], pair_recv.at[0], device_id=other, device_id_type=MESH
@@ -467,20 +498,25 @@
     def _():
         entering[...] = jnp.zeros_like(entering)
 
-    turn = jnp.where(own_stage < 2, 0, jnp.where(own_stage == 2, 1, 3))
-
-    @pl.loop(0, LOCAL)
+    turn = jnp.where(own_stage < 2, 0, 1)
+
+    @pl.loop(0, LOCAL - 1)
     def _(m):
-        @pl.when(m == turn)
+        @pl.when((own_stage < LOCAL - 1) & (m == turn))
         def _():
             run_pair()
 
         local_output(m)
 
-        @pl.when(m > 0)
-        def _():
-            send_outputs(m - 1)
-
+    @pl.when(own_stage == LOCAL - 1)
+    def _():
+        run_pair()
+
+    @pl.loop(0, LOCAL - 1)
+    def _(m):
+        send_outputs(m)
+
+    local_output(LOCAL - 1)
     send_outputs(LOCAL - 1)
 
     column = jnp.broadcast_to(slots.astype(F32), (128, TOK)).T[:, 0:1].astype(jnp.int32)
@@ -560,6 +596,8 @@
             vmem((LOCAL, D, WIDTH), BF16),
             vmem((LOCAL, D, WIDTH), BF16),
             vmem((16, D), BF16),
+            vmem((ROWS, 2 * WIDTH), F32),
+            vmem((16, ROWS), F32),
             vmem((LOCAL, ROWS, 128), F32),
             vmem((LOCAL, 16, ROWS), F32),
             vmem((LOCAL, HEADS, ROWS, 2 * K), BF16),

time: 78.4 us -> 76.6 us (0.977); the launches traced: 76.9 us -> 76.3 us
  no operation moved by 1% of the time
where the time goes in v4:
time: 76.6 us; the launch traced here: 76.3 us
  Pallas kernels  74 us (97%)
  local copies, waits for them, and re-layouts  2.3 us (3%)
    pallas_call x1, Pallas kernels, per_device(): pl.pallas_call(layer_kernel, name='layer', out_shape=jax.ShapeDtypeStruct...  74 us
    unnamed x1, local copies, waits for them, and re-layouts  2.3 us

profile of v4, /device:TPU:25, one launch (start us, length us, event | category | flops | bytes accessed | tf_op | source)
XLA Modules:
  0.0 76.3 jit_solution(9157098695897580042)
XLA Ops:
  0.0 74.0 %layer.1 = bf16[256,2048]{1,0:T(8,128)(2,1)} custom-call(f32[4,4]{1,0:T(4,128)} %rate_ref.1, s32[1,512]{1,0:T(1,128)} %bitcast.6, bf16[512,2048]{1,0:T(8,128)(2,1)} %tok_ref.1, bf16[2048,512]{1,0:T(8,128)(2,1)} %wq_ref.1, bf16[4,2048,512]{2,1,0:T(8,128)(2,1)} %wk_ref.1, bf16[4,2048,512]{2,1,0:T(8,128)(2,1)} %wv_ref.1, bf16[4,4,2048]{2,1,0:T(4,128)(2,1)} %bitcast.4, ...), custom_call_target="tpu_custom_call" | custom-call | tf_op jit(solution)/shard_map/layer/pallas_call | solution.py:580
  74.0 2.3 %copy.12 = bf16[256,2048]{1,0:T(8,128)(2,1)} copy(bf16[256,2048]{1,0:T(8,128)(2,1)} %layer.1) | data formatting | bytes 2097152

commit v5 on v4

--- a/solution.py
+++ b/solution.py
@@ -63,14 +63,10 @@
     return jnp.concatenate(parts, axis=0)
 
 
-def unit_lower_inverses(blocks, beside):
+def unit_lower_inverses(low, inverse, beside):
     beside = list(beside)
-    side = blocks[0].shape[0]
-    row, col = iota((side, side), 0), iota((side, side), 1)
-    apart = row ^ col
-    eye = ones_where(row == col)
-    low = [b.astype(BF16) for b in blocks]
-    inverse = [jnp.where(apart == 1, -b, 0.0).astype(BF16) + eye for b in blocks]
+    side = low[0].shape[0]
+    apart = iota((side, side), 0) ^ iota((side, side), 1)
     size = 2
     while size < side:
         whole = size < 16
@@ -90,7 +86,7 @@
         size *= 2
     for work in beside:
         work()
-    return inverse, eye
+    return inverse
 
 
 def three_pass(a, b):
@@ -102,9 +98,9 @@
 
 
 def layer_kernel(
-    rate_ref, routes_ref, tok_ref, wq_ref, wk_ref, wv_ref, wb_ref, wd_ref, gain_ref, wo_ref,
+    rate_ref, routes_hbm, tok_ref, wq_ref, wk_ref, wv_ref, wb_hbm, wd_hbm, gain_hbm, wo_ref,
     out_ref,
-    tok, outgoing, counts, cnt, xbuf, wq, wk, wv, gates, kv, logits_s, total_s, total_ts, keys_s, solved_hi,
+    routes_ref, wb_ref, wd_ref, gain_ref, tok, outgoing, counts, cnt, xbuf, wq, wk, wv, gates, kv, logits_s, fades, total_ts, keys_s, solved_hi,
     solved_lo, mw, maps, states, entering, base, reach, reply, returned, picked, partner, wo,
     w_other,
     load_sem, wkv_sem, own_sem, x_send, x_recv, c_send, c_recv, f_send, f_recv,
@@ -123,7 +119,16 @@
         return lax.rem(m + 2 * half, LOCAL) * 4 + h
 
     tok_load = pltpu.make_async_copy(tok_ref.at[:, mine], tok, load_sem.at[0])
+    routes_load = pltpu.make_async_copy(routes_hbm, routes_ref, load_sem.at[3])
+    routes_load.start()
     tok_load.start()
+    small_loads = [
+        pltpu.make_async_copy(wb_hbm, wb_ref, load_sem.at[4]),
+        pltpu.make_async_copy(wd_hbm, wd_ref, load_sem.at[5]),
+        pltpu.make_async_copy(gain_hbm, gain_ref, load_sem.at[6]),
+    ]
+    for load in small_loads:
+        load.start()
     barrier = pltpu.get_barrier_semaphore()
     for d in range(1, MEM):
         pl.semaphore_signal(
@@ -141,6 +146,7 @@
             pltpu.make_async_copy(wv_ref.at[m], wv.at[m], wkv_sem.at[1, m]),
         )
 
+    routes_load.wait()
     route = routes_ref[...]
     member = (iota((MEM * LOCAL, TOK), 0) == route).astype(F32)
     upper_tok = ones_where(iota((TOK, TOK), 0) <= iota((TOK, TOK), 1))
@@ -249,11 +255,20 @@
             device_id={"ctx": owner(m, h)}, device_id_type=MESH,
         )
 
-    def fade_of(g_col, g_row):
-        lower = iota((ROWS, ROWS), 0) >= iota((ROWS, ROWS), 1)
-        return jnp.where(lower, jnp.exp(jnp.where(lower, g_col - g_row, 0.0)), 0.0)
-
     gates[...] = jnp.zeros_like(gates)
+    for load in small_loads:
+        load.wait()
+    square = iota((K, K), 0), iota((K, K), 1)
+    none = jnp.zeros((K, K), BF16)
+
+    def block_lower(first, below, second):
+        return jnp.concatenate(
+            [
+                jnp.concatenate([first, none], axis=1),
+                jnp.concatenate([below, second], axis=1),
+            ],
+            axis=0,
+        )
 
     def wait_tokens(m):
         for copy in weights(m):
@@ -307,15 +322,23 @@
         low = (forget - hi.astype(F32) - mid.astype(F32)).astype(BF16)
         total_t = mm(hi, upper) + mm(mid, upper) + mm(low, upper)
         both_t = jnp.where(gate < HEADS, strength, total_t)
-        both = jnp.concatenate([both_t, jnp.zeros((112, ROWS), F32)], axis=0).T
         total_ts[m] = both_t
-        total_s[m] = both
+        b_hi, b_mid = split(both_t)
+        b_low = (both_t - b_hi.astype(F32) - b_mid.astype(F32)).astype(BF16)
+        at_gate = iota((48, 2 * WIDTH), 0) & 15
+        wide = lax.dot_general(
+            jnp.concatenate([b_hi, b_mid, b_low], axis=0),
+            ones_where(at_gate == iota((48, 2 * WIDTH), 1) // K),
+            (((0,), (0,)), ((), ())),
+            preferred_element_type=F32,
+        )
+        fades[m] = wide[:, WIDTH:]
 
         keys, corner, target = [None] * HEADS, [None] * HEADS, [None] * HEADS
-        blocks = [None] * (2 * HEADS)
-        last = both[ROWS - 1 : ROWS, :]
-        square = iota((K, K), 0), iota((K, K), 1)
+        blocks, inverse = [None] * (2 * HEADS), [None] * (2 * HEADS)
         strict = square[0] > square[1]
+        pair = (square[0] ^ square[1]) == 1
+        eye = ones_where(square[0] == square[1])
         for h in heads:
             at = slice(h * K, (h + 1) * K)
             k = unit(keys_all[:, at])
@@ -326,15 +349,16 @@
             gram = mm_nt(
                 jnp.concatenate([k_hi, k_lo], axis=1), jnp.concatenate([k_hi, k_hi], axis=1)
             ) + mm_nt(k_hi, k_lo)
-            g_col = both[:, HEADS + h : HEADS + h + 1]
+            beta = wide[:, at]
+            g_col = wide[:, WIDTH + h * K : WIDTH + (h + 1) * K]
             g_row = both_t[HEADS + h : HEADS + h + 1, :]
-            beta = both[:, h : h + 1]
             for b in range(2):
                 part = slice(b * K, (b + 1) * K)
                 gap = jnp.minimum(g_col[part] - g_row[:, part], 0.0)
-                mix = gram[part, part] * jnp.exp(gap) * beta[part]
-                blocks[2 * h + b] = jnp.where(strict, mix, 0.0)
-            corner[h] = gram[K:, :K] * jnp.exp(g_col[K:] - g_row[:, :K]) * beta[K:]
+                mix = jnp.where(strict, gram[part, part] * jnp.exp(gap) * beta[part], 0.0)
+                blocks[2 * h + b] = split(mix)
+                inverse[2 * h + b] = jnp.where(pair, -mix, 0.0).astype(BF16) + eye
+            corner[h] = split(gram[K:, :K] * jnp.exp(g_col[K:] - g_row[:, :K]) * beta[K:])
             target[h] = jnp.concatenate(
                 [(beta * jnp.exp(g_col)) * k, beta * values_all[:, at]], axis=1
             )
@@ -342,47 +366,30 @@
         if following is not None:
             wait_tokens(following)
             beside = projections(following)
-        inverse, eye = unit_lower_inverses(blocks, beside)
-        none = jnp.zeros((K, K), BF16)
-        cross = [
-            mm(corner[h].astype(BF16), inverse[2 * h]).astype(BF16) for h in heads
-        ]
+        inverse = unit_lower_inverses([b[0] for b in blocks], inverse, beside)
+        cross = [mm(corner[h][0], inverse[2 * h]).astype(BF16) for h in heads]
         cross = [mm(inverse[2 * h + 1], cross[h]).astype(BF16) for h in heads]
         inverse = [
-            jnp.concatenate(
-                [
-                    jnp.concatenate([inverse[2 * h] - eye, none], axis=1),
-                    jnp.concatenate([-cross[h], inverse[2 * h + 1] - eye], axis=1),
-                ],
-                axis=0,
+            block_lower(inverse[2 * h] - eye, -cross[h], inverse[2 * h + 1] - eye) for h in heads
+        ]
+        shift = [mm(inverse[h], target[h].astype(BF16)) for h in heads]
+        guess = [target[h] + shift[h] for h in heads]
+        rest = [None] * HEADS
+        for h in heads:
+            mix = tuple(
+                block_lower(blocks[2 * h][i], corner[h][i], blocks[2 * h + 1][i]) for i in range(2)
             )
-            for h in heads
-        ]
-        guess = [target[h] + mm(inverse[h], target[h].astype(BF16)) for h in heads]
-        rest = [None] * HEADS
-        for h in heads:
-            a_hi, a_lo = split(blocks[2 * h])
-            b_hi, b_lo = split(blocks[2 * h + 1])
-            c_hi, c_lo = split(corner[h])
-            mix_hi = jnp.concatenate(
-                [jnp.concatenate([a_hi, none], axis=1), jnp.concatenate([c_hi, b_hi], axis=1)],
-                axis=0,
-            )
-            mix_lo = jnp.concatenate(
-                [jnp.concatenate([a_lo, none], axis=1), jnp.concatenate([c_lo, b_lo], axis=1)],
-                axis=0,
-            )
-            rest[h] = target[h] - guess[h] - three_pass((mix_hi, mix_lo), split(guess[h]))
+            rest[h] = -(shift[h] + three_pass(mix, split(guess[h])))
         solved = [
-            guess[h] + rest[h] + mm(inverse[h], rest[h].astype(BF16)) for h in heads
+            guess[h] + (rest[h] + mm(inverse[h], rest[h].astype(BF16))) for h in heads
         ]
         diagonal = square[0] == square[1]
         for h in heads:
             y = split(solved[h])
             solved_hi[m, h], solved_lo[m, h] = y
-            g_last = last[:, HEADS + h : HEADS + h + 1]
-            tail = keys[h] * jnp.exp(g_last - both[:, HEADS + h : HEADS + h + 1])
-            out = three_pass(split(tail.T), y)
+            g_col = fades[m, :, h * K : (h + 1) * K]
+            g_last = g_col[ROWS - 1 : ROWS, :]
+            out = three_pass(split((keys[h] * jnp.exp(g_last - g_col)).T), y)
             p = m * HEADS + h
             mw[p, :, :K] = (jnp.where(diagonal, jnp.exp(g_last), 0.0) - out[:, :K]).astype(BF16)
             mw[p, :, K:] = out[:, K:].astype(BF16)
@@ -410,17 +417,24 @@
 
     def local_output(m):
         query_all = mm(xbuf[m], wq[...])
-        both = total_s[m]
-        for h in heads:
-            q = unit(query_all[:, h * K : (h + 1) * K])
+        lower = square[0] >= square[1]
+        for h in heads:
+            at = slice(h * K, (h + 1) * K)
+            q = unit(query_all[:, at])
             q_hi, q_lo = split(q)
             k_hi, k_lo = keys_s[m, h, :, :K], keys_s[m, h, :, K:]
             gram = mm_nt(
                 jnp.concatenate([q_hi, q_lo], axis=1), jnp.concatenate([k_hi, k_hi], axis=1)
             ) + mm_nt(q_hi, k_lo)
-            g_col = both[:, HEADS + h : HEADS + h + 1]
+            g_col = fades[m, :, at]
             g_row = total_ts[m, HEADS + h : HEADS + h + 1, :]
-            scores = split(gram * fade_of(g_col, g_row))
+            parts = []
+            for b in range(2):
+                part = slice(b * K, (b + 1) * K)
+                gap = jnp.minimum(g_col[part] - g_row[:, part], 0.0)
+                parts.append(split(jnp.where(lower, gram[part, part] * jnp.exp(gap), 0.0)))
+            below = split(gram[K:, :K] * jnp.exp(g_col[K:] - g_row[:, :K]))
+            scores = tuple(block_lower(parts[0][i], below[i], parts[1][i]) for i in range(2))
             out = three_pass(scores, (solved_hi[m, h], solved_lo[m, h]))
             base[m, :, h * K : (h + 1) * K] = out[:, K:]
             r_hi, r_lo = split(q * jnp.exp(g_col) - out[:, :K])
@@ -508,12 +522,12 @@
 
         local_output(m)
 
-    @pl.when(own_stage == LOCAL - 1)
-    def _():
-        run_pair()
-
     @pl.loop(0, LOCAL - 1)
     def _(m):
+        @pl.when((own_stage == LOCAL - 1) & (m == LOCAL - 2))
+        def _():
+            run_pair()
+
         send_outputs(m)
 
     local_output(LOCAL - 1)
@@ -582,11 +596,15 @@
         name="layer",
         out_shape=jax.ShapeDtypeStruct((TOK // 2, D), BF16),
         in_specs=[
-            pl.BlockSpec(memory_space=pltpu.SMEM), in_vmem, in_place, in_place, in_place,
-            in_place, in_vmem, in_vmem, in_vmem, in_place,
+            pl.BlockSpec(memory_space=pltpu.SMEM), in_place, in_place, in_place, in_place,
+            in_place, in_place, in_place, in_place, in_place,
         ],
         out_specs=in_vmem,
         scratch_shapes=[
+            vmem((1, TOK), jnp.int32),
+            vmem((LOCAL, HEADS, D), BF16),
+            vmem((LOCAL, HEADS, D), BF16),
+            vmem((1, WIDTH), F32),
             vmem((TOK, DH), BF16),
             vmem((LOCAL, MEM, CAP, DH), BF16),
             vmem((MEM, 8, 128), F32),
@@ -598,7 +616,7 @@
             vmem((16, D), BF16),
             vmem((ROWS, 2 * WIDTH), F32),
             vmem((16, ROWS), F32),
-            vmem((LOCAL, ROWS, 128), F32),
+            vmem((LOCAL, ROWS, WIDTH), F32),
             vmem((LOCAL, 16, ROWS), F32),
             vmem((LOCAL, HEADS, ROWS, 2 * K), BF16),
             vmem((LOCAL, HEADS, ROWS, 2 * K), BF16),
@@ -615,7 +633,7 @@
             vmem((TOK // 2, WIDTH), BF16),
             vmem((WIDTH, D), BF16),
             vmem((WIDTH, D), BF16),
-            dma((3,)), dma((2, LOCAL)), dma((LOCAL,)),
+            dma((7,)), dma((2, LOCAL)), dma((LOCAL,)),
             dma((MEM, LOCAL)), dma((MEM, LOCAL)), dma((MEM,)), dma((MEM,)),
             dma((MEM, LOCAL)), dma((MEM, LOCAL)),
             dma((CTX,)), dma((CTX,)), dma((CTX,)), dma((CTX,)),

time: 76.6 us -> 76.7 us (level)
  the two profiles are of different devices: /device:TPU:25 before, /device:TPU:41 now
where the time goes in v5:
time: 76.7 us; the launch traced here: 76.5 us
  Pallas kernels  74.2 us (97%)
  local copies, waits for them, and re-layouts  2.3 us (3%)
    pallas_call x1, Pallas kernels, per_device(): pl.pallas_call(layer_kernel, name='layer', out_shape=jax.ShapeDtypeStruct...  74.2 us
    unnamed x1, local copies, waits for them, and re-layouts  2.3 us

profile of v5, /device:TPU:41, one launch (start us, length us, event | category | flops | bytes accessed | tf_op | source)
XLA Modules:
  0.0 76.5 jit_solution(11149511313394660612)
XLA Ops:
  0.0 74.2 %layer.1 = bf16[256,2048]{1,0:T(8,128)(2,1)} custom-call(f32[4,4]{1,0:T(4,128)} %rate_ref.1, s32[1,512]{1,0:T(1,128)} %bitcast.6, bf16[512,2048]{1,0:T(8,128)(2,1)} %tok_ref.1, bf16[2048,512]{1,0:T(8,128)(2,1)} %wq_ref.1, bf16[4,2048,512]{2,1,0:T(8,128)(2,1)} %wk_ref.1, bf16[4,2048,512]{2,1,0:T(8,128)(2,1)} %wv_ref.1, bf16[4,4,2048]{2,1,0:T(4,128)(2,1)} %bitcast.4, ...), custom_call_target="tpu_custom_call" | custom-call | tf_op jit(solution)/shard_map/layer/pallas_call | solution.py:594
  74.2 2.3 %copy.12 = bf16[256,2048]{1,0:T(8,128)(2,1)} copy(bf16[256,2048]{1,0:T(8,128)(2,1)} %layer.1) | data formatting | bytes 2097152

commit v6 on v5

--- a/solution.py
+++ b/solution.py
@@ -226,7 +226,6 @@
     @pl.loop(1, LOCAL)
     def _(m):
         gather(m)
-        launch(m)
         for copy in weights(m):
             copy.start()
 
@@ -239,6 +238,13 @@
         for d in (1, 3, 2):
             x_arrival(d, m).wait_recv()
             forward(d, m).start()
+
+    for d in range(1, MEM):
+        x_copy(d, 0).wait_send()
+
+    @pl.loop(1, LOCAL)
+    def _(m):
+        launch(m)
 
     pass_on(0)
     for d in range(1, MEM):
@@ -259,13 +265,22 @@
     for load in small_loads:
         load.wait()
     square = iota((K, K), 0), iota((K, K), 1)
-    none = jnp.zeros((K, K), BF16)
-
-    def block_lower(first, below, second):
+
+    def lower_times(matrix, right):
+        first, below, second = matrix
+        return jnp.concatenate(
+            [mm(first, right[:K]), mm(jnp.concatenate([below, second], axis=1), right)], axis=0
+        )
+
+    def lower_times_exact(matrix, right):
+        first, below, second = matrix
+        r_hi, r_lo = right
         return jnp.concatenate(
             [
-                jnp.concatenate([first, none], axis=1),
-                jnp.concatenate([below, second], axis=1),
+                three_pass(first, (r_hi[:K], r_lo[:K])),
+                three_pass(
+                    tuple(jnp.concatenate([below[i], second[i]], axis=1) for i in range(2)), right
+                ),
             ],
             axis=0,
         )
@@ -370,18 +385,16 @@
         cross = [mm(corner[h][0], inverse[2 * h]).astype(BF16) for h in heads]
         cross = [mm(inverse[2 * h + 1], cross[h]).astype(BF16) for h in heads]
         inverse = [
-            block_lower(inverse[2 * h] - eye, -cross[h], inverse[2 * h + 1] - eye) for h in heads
+            (inverse[2 * h] - eye, -cross[h], inverse[2 * h + 1] - eye) for h in heads
         ]
-        shift = [mm(inverse[h], target[h].astype(BF16)) for h in heads]
+        shift = [lower_times(inverse[h], target[h].astype(BF16)) for h in heads]
         guess = [target[h] + shift[h] for h in heads]
         rest = [None] * HEADS
         for h in heads:
-            mix = tuple(
-                block_lower(blocks[2 * h][i], corner[h][i], blocks[2 * h + 1][i]) for i in range(2)
-            )
-            rest[h] = -(shift[h] + three_pass(mix, split(guess[h])))
+            mix = (blocks[2 * h], corner[h], blocks[2 * h + 1])
+            rest[h] = -(shift[h] + lower_times_exact(mix, split(guess[h])))
         solved = [
-            guess[h] + (rest[h] + mm(inverse[h], rest[h].astype(BF16))) for h in heads
+            guess[h] + (rest[h] + lower_times(inverse[h], rest[h].astype(BF16))) for h in heads
         ]
         diagonal = square[0] == square[1]
         for h in heads:
@@ -399,6 +412,47 @@
             def _():
                 map_copy(m, h).start()
 
+    def state_copy(to):
+        return pltpu.make_async_remote_copy(
+            states.at[to], entering.at[own_pair], state_send.at[to], state_recv.at[own_pair],
+            device_id={"ctx": to}, device_id_type=MESH,
+        )
+
+    def run_pair():
+        maps[c] = mw[own_pair]
+        for j in range(CTX - 1):
+
+            @pl.when(c != j)
+            def _():
+                pltpu.make_async_remote_copy(
+                    mw.at[j], maps.at[j], map_send.at[j], map_recv.at[j],
+                    device_id={"ctx": j}, device_id_type=MESH,
+                ).wait_recv()
+
+        state = maps[0, :, K:].astype(F32)
+        states[1] = state.astype(BF16)
+        for j in range(1, CTX - 1):
+            step = maps[j, :, :K]
+            s_hi, s_lo = split(state)
+            state = maps[j, :, K:].astype(F32) + mm(
+                jnp.concatenate([step, step], axis=1), jnp.concatenate([s_hi, s_lo], axis=0)
+            )
+            states[j + 1] = state.astype(BF16)
+
+        @pl.loop(1, CTX)
+        def _(j):
+            @pl.when(c != j)
+            def _():
+                state_copy(j).start()
+
+        @pl.when(c > 0)
+        def _():
+            entering[own_pair] = states[c]
+
+    @pl.when(c == 0)
+    def _():
+        entering[...] = jnp.zeros_like(entering)
+
     wait_tokens(0)
     for work in projections(0):
         work()
@@ -406,6 +460,10 @@
     @pl.loop(0, LOCAL - 1)
     def _(m):
         make_maps(m, m + 1)
+
+    @pl.when(own_stage < 2)
+    def _():
+        run_pair()
 
     make_maps(LOCAL - 1, None)
 
@@ -434,49 +492,13 @@
                 gap = jnp.minimum(g_col[part] - g_row[:, part], 0.0)
                 parts.append(split(jnp.where(lower, gram[part, part] * jnp.exp(gap), 0.0)))
             below = split(gram[K:, :K] * jnp.exp(g_col[K:] - g_row[:, :K]))
-            scores = tuple(block_lower(parts[0][i], below[i], parts[1][i]) for i in range(2))
-            out = three_pass(scores, (solved_hi[m, h], solved_lo[m, h]))
+            out = lower_times_exact(
+                (parts[0], below, parts[1]), (solved_hi[m, h], solved_lo[m, h])
+            )
             base[m, :, h * K : (h + 1) * K] = out[:, K:]
             r_hi, r_lo = split(q * jnp.exp(g_col) - out[:, :K])
             reach[m, :, 2 * h * K : (2 * h + 1) * K] = r_hi
             reach[m, :, (2 * h + 1) * K : (2 * h + 2) * K] = r_lo
-
-    def state_copy(to):
-        return pltpu.make_async_remote_copy(
-            states.at[to], entering.at[own_pair], state_send.at[to], state_recv.at[own_pair],
-            device_id={"ctx": to}, device_id_type=MESH,
-        )
-
-    def run_pair():
-        maps[c] = mw[own_pair]
-        state = None
-        for j in range(CTX - 1):
-
-            @pl.when(c != j)
-            def _():
-                pltpu.make_async_remote_copy(
-                    mw.at[j], maps.at[j], map_send.at[j], map_recv.at[j],
-                    device_id={"ctx": j}, device_id_type=MESH,
-                ).wait_recv()
-
-            add = maps[j, :, K:].astype(F32)
-            if j == 0:
-                state = add
-            else:
-                step = maps[j, :, :K]
-                s_hi, s_lo = split(state)
-                state = add + mm(
-                    jnp.concatenate([step, step], axis=1), jnp.concatenate([s_hi, s_lo], axis=0)
-                )
-            states[j + 1] = state.astype(BF16)
-
-            @pl.when(c != j + 1)
-            def _():
-                state_copy(j + 1).start()
-
-            @pl.when(c == j + 1)
-            def _():
-                entering[own_pair] = states[j + 1]
 
     def ret_copy(d, m):
         to = lax.rem(z + d, MEM)
@@ -508,30 +530,14 @@
         for d in (2, 1, 3):
             ret_copy(d, m).start()
 
-    @pl.when(c == 0)
-    def _():
-        entering[...] = jnp.zeros_like(entering)
-
-    turn = jnp.where(own_stage < 2, 0, 1)
-
-    @pl.loop(0, LOCAL - 1)
+    @pl.loop(0, LOCAL)
     def _(m):
-        @pl.when((own_stage < LOCAL - 1) & (m == turn))
+        @pl.when((own_stage > 1) & (m == 2 * own_stage - 3))
         def _():
             run_pair()
 
         local_output(m)
-
-    @pl.loop(0, LOCAL - 1)
-    def _(m):
-        @pl.when((own_stage == LOCAL - 1) & (m == LOCAL - 2))
-        def _():
-            run_pair()
-
         send_outputs(m)
-
-    local_output(LOCAL - 1)
-    send_outputs(LOCAL - 1)
 
     column = jnp.broadcast_to(slots.astype(F32), (128, TOK)).T[:, 0:1].astype(jnp.int32)
 
@@ -567,8 +573,12 @@
     @pl.loop(0, LOCAL)
     def _(m):
         for d in range(1, MEM):
-            x_copy(d, m).wait_send()
             ret_copy(d, m).wait_send()
+
+            @pl.when(m > 0)
+            def _():
+                x_copy(d, m).wait_send()
+
         for d in range(MEM):
             forward(d, m).wait_send()
         for h in heads:

time: 76.7 us -> 82.1 us (1.070)
  the two profiles are of different devices: /device:TPU:41 before, /device:TPU:25 now
where the time goes in v6:
time: 82.1 us; the launch traced here: 81.5 us
  Pallas kernels  79.1 us (96%)
  local copies, waits for them, and re-layouts  2.3 us (3%)
    pallas_call x1, Pallas kernels, per_device(): pl.pallas_call(layer_kernel, name='layer', out_shape=jax.ShapeDtypeStruct...  79.1 us
    unnamed x1, local copies, waits for them, and re-layouts  2.3 us

profile of v6, /device:TPU:25, one launch (start us, length us, event | category | flops | bytes accessed | tf_op | source)
XLA Modules:
  0.0 81.5 jit_solution(15877230119290985758)
XLA Ops:
  0.0 79.1 %layer.1 = bf16[256,2048]{1,0:T(8,128)(2,1)} custom-call(f32[4,4]{1,0:T(4,128)} %rate_ref.1, s32[1,512]{1,0:T(1,128)} %bitcast.6, bf16[512,2048]{1,0:T(8,128)(2,1)} %tok_ref.1, bf16[2048,512]{1,0:T(8,128)(2,1)} %wq_ref.1, bf16[4,2048,512]{2,1,0:T(8,128)(2,1)} %wk_ref.1, bf16[4,2048,512]{2,1,0:T(8,128)(2,1)} %wv_ref.1, bf16[4,4,2048]{2,1,0:T(4,128)(2,1)} %bitcast.4, ...), custom_call_target="tpu_custom_call" | custom-call | tf_op jit(solution)/shard_map/layer/pallas_call | solution.py:604
  79.2 2.3 %copy.12 = bf16[256,2048]{1,0:T(8,128)(2,1)} copy(bf16[256,2048]{1,0:T(8,128)(2,1)} %layer.1) | data formatting | bytes 2097152

commit v7 on v6

--- a/solution.py
+++ b/solution.py
@@ -226,6 +226,7 @@
     @pl.loop(1, LOCAL)
     def _(m):
         gather(m)
+        launch(m)
         for copy in weights(m):
             copy.start()
 
@@ -238,13 +239,6 @@
         for d in (1, 3, 2):
             x_arrival(d, m).wait_recv()
             forward(d, m).start()
-
-    for d in range(1, MEM):
-        x_copy(d, 0).wait_send()
-
-    @pl.loop(1, LOCAL)
-    def _(m):
-        launch(m)
 
     pass_on(0)
     for d in range(1, MEM):
@@ -429,15 +423,34 @@
                     device_id={"ctx": j}, device_id_type=MESH,
                 ).wait_recv()
 
-        state = maps[0, :, K:].astype(F32)
-        states[1] = state.astype(BF16)
-        for j in range(1, CTX - 1):
+        pairs = []
+        for j in range(0, CTX - 2, 2):
+            joined = mm(maps[j + 1, :, :K], maps[j])
+            m_hi, m_lo = split(joined[:, :K])
+            pairs.append(
+                (
+                    jnp.concatenate([m_hi, m_lo, m_hi], axis=1),
+                    joined[:, K:] + maps[j + 1, :, K:].astype(F32),
+                )
+            )
+        states[1] = maps[0, :, K:]
+        state = pairs[0][1]
+        even = [state]
+        for step, add in pairs[1:]:
+            s_hi, s_lo = split(state)
+            state = add + mm(step, jnp.concatenate([s_hi, s_hi, s_lo], axis=0))
+            even.append(state)
+        for n, state in enumerate(even):
+            j = 2 * n + 2
+            s_hi, s_lo = split(state)
+            states[j] = s_hi
             step = maps[j, :, :K]
-            s_hi, s_lo = split(state)
-            state = maps[j, :, K:].astype(F32) + mm(
-                jnp.concatenate([step, step], axis=1), jnp.concatenate([s_hi, s_lo], axis=0)
-            )
-            states[j + 1] = state.astype(BF16)
+            states[j + 1] = (
+                maps[j, :, K:].astype(F32)
+                + mm(
+                    jnp.concatenate([step, step], axis=1), jnp.concatenate([s_hi, s_lo], axis=0)
+                )
+            ).astype(BF16)
 
         @pl.loop(1, CTX)
         def _(j):
@@ -461,7 +474,7 @@
     def _(m):
         make_maps(m, m + 1)
 
-    @pl.when(own_stage < 2)
+    @pl.when(own_stage == 0)
     def _():
         run_pair()
 
@@ -530,13 +543,23 @@
         for d in (2, 1, 3):
             ret_copy(d, m).start()
 
-    @pl.loop(0, LOCAL)
+    @pl.loop(0, LOCAL - 1)
     def _(m):
-        @pl.when((own_stage > 1) & (m == 2 * own_stage - 3))
+        @pl.when((m < 2) & (own_stage == m + 1))
         def _():
             run_pair()
 
         local_output(m)
+
+    send_outputs(0)
+    local_output(LOCAL - 1)
+
+    @pl.loop(1, LOCAL)
+    def _(m):
+        @pl.when((m == 2) & (own_stage == LOCAL - 1))
+        def _():
+            run_pair()
+
         send_outputs(m)
 
     column = jnp.broadcast_to(slots.astype(F32), (128, TOK)).T[:, 0:1].astype(jnp.int32)
@@ -573,12 +596,8 @@
     @pl.loop(0, LOCAL)
     def _(m):
         for d in range(1, MEM):
+            x_copy(d, m).wait_send()
             ret_copy(d, m).wait_send()
-
-            @pl.when(m > 0)
-            def _():
-                x_copy(d, m).wait_send()
-
         for d in range(MEM):
             forward(d, m).wait_send()
         for h in heads:

time: 82.1 us -> 75.4 us (0.918)
  Pallas kernels: 79.1 us -> 71.7 us
    pallas_call x1, Pallas kernels: 79.1 us -> 71.7 us  [per_device(): pl.pallas_call(layer_kernel, name='layer', out_shape=jax.ShapeDtypeStruct...]
where the time goes in v7:
time: 75.4 us; the launch traced here: 74 us
  Pallas kernels  71.7 us (95%)
  local copies, waits for them, and re-layouts  2.3 us (3%)
    pallas_call x1, Pallas kernels, per_device(): pl.pallas_call(layer_kernel, name='layer', out_shape=jax.ShapeDtypeStruct...  71.7 us
    unnamed x1, local copies, waits for them, and re-layouts  2.3 us

profile of v7, /device:TPU:25, one launch (start us, length us, event | category | flops | bytes accessed | tf_op | source)
XLA Modules:
  0.0 74.0 jit_solution(12200018632999941607)
XLA Ops:
  0.0 71.7 %layer.1 = bf16[256,2048]{1,0:T(8,128)(2,1)} custom-call(f32[4,4]{1,0:T(4,128)} %rate_ref.1, s32[1,512]{1,0:T(1,128)} %bitcast.6, bf16[512,2048]{1,0:T(8,128)(2,1)} %tok_ref.1, bf16[2048,512]{1,0:T(8,128)(2,1)} %wq_ref.1, bf16[4,2048,512]{2,1,0:T(8,128)(2,1)} %wk_ref.1, bf16[4,2048,512]{2,1,0:T(8,128)(2,1)} %wv_ref.1, bf16[4,4,2048]{2,1,0:T(4,128)(2,1)} %bitcast.4, ...), custom_call_target="tpu_custom_call" | custom-call | tf_op jit(solution)/shard_map/layer/pallas_call | solution.py:623
  71.7 2.3 %copy.12 = bf16[256,2048]{1,0:T(8,128)(2,1)} copy(bf16[256,2048]{1,0:T(8,128)(2,1)} %layer.1) | data formatting | bytes 2097152

commit v8 on v7

--- a/solution.py
+++ b/solution.py
@@ -400,7 +400,8 @@
             p = m * HEADS + h
             mw[p, :, :K] = (jnp.where(diagonal, jnp.exp(g_last), 0.0) - out[:, :K]).astype(BF16)
             mw[p, :, K:] = out[:, K:].astype(BF16)
-        for h in heads:
+        for turn in heads:
+            h = lax.rem(c + turn, HEADS)
 
             @pl.when((m * HEADS + h != own_pair) & (c < CTX - 1))
             def _():
@@ -453,10 +454,12 @@
             ).astype(BF16)
 
         @pl.loop(1, CTX)
-        def _(j):
-            @pl.when(c != j)
+        def _(turn):
+            to = lax.rem(c + turn, CTX)
+
+            @pl.when(to > 0)
             def _():
-                state_copy(j).start()
+                state_copy(to).start()
 
         @pl.when(c > 0)
         def _():
@@ -613,6 +616,10 @@
             state_copy(j).wait_send()
 
 
+def hand_over(mixed_ref, out_ref):
+    out_ref[...] = mixed_ref[...]
+
+
 def per_device(
     tokens, routes, w_query, w_key, w_value, w_beta, w_decay, decay_rate, norm_gain, w_out
 ):
@@ -620,7 +627,7 @@
     vmem = pltpu.VMEM
     in_vmem = pl.BlockSpec(memory_space=pltpu.VMEM)
     in_place = pl.BlockSpec(memory_space=pl.ANY)
-    return pl.pallas_call(
+    mixed = pl.pallas_call(
         layer_kernel,
         name="layer",
         out_shape=jax.ShapeDtypeStruct((TOK // 2, D), BF16),
@@ -683,6 +690,15 @@
         norm_gain.reshape(1, WIDTH),
         w_out,
     )
+    rows = pl.BlockSpec((TOK // 8, D), lambda i: (i, 0))
+    return pl.pallas_call(
+        hand_over,
+        name="hand_over",
+        grid=(4,),
+        out_shape=jax.ShapeDtypeStruct((TOK // 2, D), BF16),
+        in_specs=[rows],
+        out_specs=rows,
+    )(mixed)
 
 
 def solution(mesh):

time: 75.4 us -> 77.1 us (1.023)
  the two profiles are of different devices: /device:TPU:25 before, /device:TPU:39 now
where the time goes in v8:
time: 77.1 us; the launch traced here: 76.9 us
  Pallas kernels  76.9 us (100%)
    pallas_call x1, Pallas kernels, per_device(): pl.pallas_call(layer_kernel, name='layer', out_shape=jax.ShapeDtypeStruct...  73.5 us
    pallas_call x1, Pallas kernels, per_device(): pl.pallas_call(hand_over, name='hand_over', grid=(4,), out_shape=jax.Shap...  3.37 us

profile of v8, /device:TPU:39, one launch (start us, length us, event | category | flops | bytes accessed | tf_op | source)
XLA Modules:
  0.0 76.9 jit_solution(9260002089673159801)
XLA Ops:
  0.0 73.5 %layer.1.mixed_ref = bf16[256,2048]{1,0:T(8,128)(2,1)} custom-call(f32[4,4]{1,0:T(4,128)} %rate_ref.1, s32[1,512]{1,0:T(1,128)} %bitcast.6, bf16[512,2048]{1,0:T(8,128)(2,1)} %tok_ref.1, bf16[2048,512]{1,0:T(8,128)(2,1)} %wq_ref.1, bf16[4,2048,512]{2,1,0:T(8,128)(2,1)} %wk_ref.1, bf16[4,2048,512]{2,1,0:T(8,128)(2,1)} %wv_ref.1, bf16[4,4,2048]{2,1,0:T(4,128)(2,1)} %bitcast.4, ...), custom_call_target="tpu_custom_call" | custom-call | tf_op jit(solution)/shard_map/layer/pallas_call | solution.py:630
  73.5 3.4 %hand_over.1 = bf16[256,2048]{1,0:T(8,128)(2,1)} custom-call(bf16[256,2048]{1,0:T(8,128)(2,1)} %layer.1.mixed_ref), custom_call_target="tpu_custom_call" | custom-call | tf_op jit(solution)/shard_map/hand_over/pallas_call | solution.py:694

commit v9 on v7

--- a/solution.py
+++ b/solution.py
@@ -112,11 +112,11 @@
     other = {"half": 1 - half}
     mine = aligned(half, DH)
     heads = range(HEADS)
-    own_stage = lax.rem(c // 4 + 2 * half, LOCAL)
+    own_stage = lax.rem(c // 4 + 4 - lax.rem(c, 4) + 2 * half, LOCAL)
     own_pair = own_stage * HEADS + lax.rem(c, 4)
 
     def owner(m, h):
-        return lax.rem(m + 2 * half, LOCAL) * 4 + h
+        return lax.rem(m + h + 2 * half, LOCAL) * 4 + h
 
     tok_load = pltpu.make_async_copy(tok_ref.at[:, mine], tok, load_sem.at[0])
     routes_load = pltpu.make_async_copy(routes_hbm, routes_ref, load_sem.at[3])
@@ -209,7 +209,7 @@
         outgoing[m] = rows.reshape(MEM, CAP, DH)
 
     def launch(m):
-        for d in (2, 1, 3):
+        for d in (1, 3, 2):
             x_copy(d, m).start()
         forward(0, m).start()
         own_copy(m).start()
@@ -400,7 +400,8 @@
             p = m * HEADS + h
             mw[p, :, :K] = (jnp.where(diagonal, jnp.exp(g_last), 0.0) - out[:, :K]).astype(BF16)
             mw[p, :, K:] = out[:, K:].astype(BF16)
-        for h in heads:
+        for turn in heads:
+            h = lax.rem(c + turn, HEADS)
 
             @pl.when((m * HEADS + h != own_pair) & (c < CTX - 1))
             def _():
@@ -453,10 +454,12 @@
             ).astype(BF16)
 
         @pl.loop(1, CTX)
-        def _(j):
-            @pl.when(c != j)
+        def _(turn):
+            to = lax.rem(c + turn, CTX)
+
+            @pl.when(to > 0)
             def _():
-                state_copy(j).start()
+                state_copy(to).start()
 
         @pl.when(c > 0)
         def _():
@@ -545,11 +548,15 @@
 
     @pl.loop(0, LOCAL - 1)
     def _(m):
-        @pl.when((m < 2) & (own_stage == m + 1))
+        @pl.when((m == 0) & (own_stage == 1))
         def _():
             run_pair()
 
         local_output(m)
+
+    @pl.when(own_stage == 2)
+    def _():
+        run_pair()
 
     send_outputs(0)
     local_output(LOCAL - 1)
@@ -623,7 +630,7 @@
     return pl.pallas_call(
         layer_kernel,
         name="layer",
-        out_shape=jax.ShapeDtypeStruct((TOK // 2, D), BF16),
+        out_shape=pltpu.VMEM((TOK // 2, D), BF16),
         in_specs=[
             pl.BlockSpec(memory_space=pltpu.SMEM), in_place, in_place, in_place, in_place,
             in_place, in_place, in_place, in_place, in_place,
@@ -669,7 +676,7 @@
             dma((MEM, LOCAL)), dma((MEM, LOCAL)), dma((2,)), dma((2,)),
         ],
         compiler_params=pltpu.CompilerParams(
-            collective_id=0, has_side_effects=True, vmem_limit_bytes=67_043_328
+            collective_id=0, has_side_effects=True, vmem_limit_bytes=58 * 1024 * 1024
         ),
     )(
         decay_rate,

time: 75.4 us -> 71.7 us (0.951)
  Pallas kernels: 71.7 us -> 69.9 us
  local copies, waits for them, and re-layouts: 2.3 us -> 0.97 us
    pallas_call x1, Pallas kernels: 71.7 us -> 69.9 us  [per_device(): pl.pallas_call(layer_kernel, name='layer', out_shape=pltpu.VMEM((TOK // 2...]
    unnamed x1, local copies, waits for them, and re-layouts: 2.3 us -> 0.97 us
where the time goes in v9:
time: 71.7 us; the launch traced here: 70.9 us
  Pallas kernels  69.9 us (97%)
  local copies, waits for them, and re-layouts  0.97 us (1%)
    pallas_call x1, Pallas kernels, per_device(): pl.pallas_call(layer_kernel, name='layer', out_shape=pltpu.VMEM((TOK // 2...  69.9 us

profile of v9, /device:TPU:25, one launch (start us, length us, event | category | flops | bytes accessed | tf_op | source)
XLA Modules:
  0.0 70.9 jit_solution(18011562433214784616)
XLA Ops:
  0.0 69.9 %layer.1 = bf16[256,2048]{1,0:T(8,128)(2,1)S(1)} custom-call(f32[4,4]{1,0:T(4,128)} %rate_ref.1, s32[1,512]{1,0:T(1,128)} %bitcast.6, bf16[512,2048]{1,0:T(8,128)(2,1)} %tok_ref.1, bf16[2048,512]{1,0:T(8,128)(2,1)} %wq_ref.1, bf16[4,2048,512]{2,1,0:T(8,128)(2,1)} %wk_ref.1, bf16[4,2048,512]{2,1,0:T(8,128)(2,1)} %wv_ref.1, bf16[4,4,2048]{2,1,0:T(4,128)(2,1)} %bitcast.4, ...), custom_call_target="tpu_custom_call" | custom-call | tf_op jit(solution)/shard_map/layer/pallas_call | solution.py:630
  69.9 1.0 %copy.12 = bf16[256,2048]{1,0:T(8,128)(2,1)} copy(bf16[256,2048]{1,0:T(8,128)(2,1)S(1)} %layer.1) | data formatting | bytes 2097152

commit v10 on v9

--- a/solution.py
+++ b/solution.py
@@ -98,9 +98,9 @@
 
 
 def layer_kernel(
-    rate_ref, routes_hbm, tok_ref, wq_ref, wk_ref, wv_ref, wb_hbm, wd_hbm, gain_hbm, wo_ref,
+    rate_hbm, routes_hbm, tok_ref, wq_ref, wk_ref, wv_ref, wb_hbm, wd_hbm, gain_hbm, wo_ref,
     out_ref,
-    routes_ref, wb_ref, wd_ref, gain_ref, tok, outgoing, counts, cnt, xbuf, wq, wk, wv, gates, kv, logits_s, fades, total_ts, keys_s, solved_hi,
+    rate_ref, routes_ref, wb_ref, wd_ref, gain_ref, tok, outgoing, counts, cnt, xbuf, wq, wk, wv, gates, kv, logits_s, fades, total_ts, keys_s, solved_hi,
     solved_lo, mw, maps, states, entering, base, reach, reply, returned, picked, partner, wo,
     w_other,
     load_sem, wkv_sem, own_sem, x_send, x_recv, c_send, c_recv, f_send, f_recv,
@@ -126,6 +126,7 @@
         pltpu.make_async_copy(wb_hbm, wb_ref, load_sem.at[4]),
         pltpu.make_async_copy(wd_hbm, wd_ref, load_sem.at[5]),
         pltpu.make_async_copy(gain_hbm, gain_ref, load_sem.at[6]),
+        pltpu.make_async_copy(rate_hbm, rate_ref, load_sem.at[7]),
     ]
     for load in small_loads:
         load.start()
@@ -320,9 +321,10 @@
         )
         live = ((iota((1, ROWS), 1) & (CAP - 1)).astype(F32) < cnt_row).astype(F32)
         gate = iota((16, 1), 0)
-        rate = jnp.zeros((16, 1), F32)
-        for h in heads:
-            rate = jnp.where(gate == HEADS + h, rate_ref[m, h], rate)
+        own_gate = iota((16, HEADS), 0) == iota((16, HEADS), 1) + HEADS
+        rate = jnp.sum(
+            jnp.where(own_gate, rate_ref[pl.ds(m, 1), :], 0.0), axis=1, keepdims=True
+        )
         strength = jax.nn.sigmoid(logits) * live
         soft = jnp.maximum(logits, 0.0) + jnp.log1p(jnp.exp(-jnp.abs(logits)))
         forget = -rate * soft * live
@@ -543,7 +545,7 @@
             scale = lax.rsqrt(jnp.mean(heads_out * heads_out, axis=1, keepdims=True) + 1e-05)
             normed = (heads_out * scale * gain_ref[:, at]).astype(BF16)
             reply[m, :, :, at] = normed.reshape(MEM, CAP, K)
-        for d in (2, 1, 3):
+        for d in (1, 3, 2):
             ret_copy(d, m).start()
 
     @pl.loop(0, LOCAL - 1)
@@ -563,28 +565,47 @@
 
     @pl.loop(1, LOCAL)
     def _(m):
-        @pl.when((m == 2) & (own_stage == LOCAL - 1))
+        @pl.when((m == 1) & (own_stage == LOCAL - 1))
         def _():
             run_pair()
 
         send_outputs(m)
 
+    for d in range(1, MEM):
+        count_copy(d).wait_send()
+
+    @pl.loop(0, LOCAL)
+    def _(m):
+        for d in range(1, MEM):
+            x_copy(d, m).wait_send()
+        for d in range(MEM):
+            forward(d, m).wait_send()
+        for h in heads:
+
+            @pl.when((m * HEADS + h != own_pair) & (c < CTX - 1))
+            def _():
+                map_copy(m, h).wait_send()
+
+    @pl.loop(1, CTX)
+    def _(j):
+        @pl.when(c != j)
+        def _():
+            state_copy(j).wait_send()
+
     column = jnp.broadcast_to(slots.astype(F32), (128, TOK)).T[:, 0:1].astype(jnp.int32)
 
-    def pick(src, rows):
-        chosen = ones_where(iota((TOK, ROWS), 1) + src * ROWS == column)
-        return mm(chosen, rows)
-
-    own_rows = jnp.concatenate([reply[m, z] for m in range(LOCAL)], axis=0)
-    total = pick(z, own_rows)
+    source = [lax.rem(z + MEM - d, MEM) for d in range(MEM)]
+    chosen = [
+        ones_where(iota((TOK, ROWS), 1) + src * ROWS == column) for src in source
+    ]
+    total = mm(chosen[0], jnp.concatenate([reply[m, z] for m in range(LOCAL)], axis=0))
     for d in (1, 3, 2):
-        src = lax.rem(z + MEM - d, MEM)
         for m in range(LOCAL):
             pltpu.make_async_remote_copy(
-                reply.at[m, z], returned.at[src, m], ret_send.at[d, m], ret_recv.at[d, m],
-                device_id={"mem": src}, device_id_type=MESH,
+                reply.at[m, z], returned.at[source[d], m], ret_send.at[d, m], ret_recv.at[d, m],
+                device_id={"mem": source[d]}, device_id_type=MESH,
             ).wait_recv()
-        total = total + pick(src, returned[src].reshape(ROWS, WIDTH))
+        total = total + mm(chosen[d], returned[source[d]].reshape(ROWS, WIDTH))
     picked[...] = total.astype(BF16)
     swap = pltpu.make_async_remote_copy(
         picked.at[aligned(1 - half, TOK // 2)], partner, pair_send.at[1], pair_recv.at[1],
@@ -597,27 +618,10 @@
     swap.wait()
     out_ref[...] = (mixed + mm(partner[...], w_other[...])).astype(BF16)
 
-    for d in range(1, MEM):
-        count_copy(d).wait_send()
-
     @pl.loop(0, LOCAL)
     def _(m):
         for d in range(1, MEM):
-            x_copy(d, m).wait_send()
             ret_copy(d, m).wait_send()
-        for d in range(MEM):
-            forward(d, m).wait_send()
-        for h in heads:
-
-            @pl.when((m * HEADS + h != own_pair) & (c < CTX - 1))
-            def _():
-                map_copy(m, h).wait_send()
-
-    @pl.loop(1, CTX)
-    def _(j):
-        @pl.when(c != j)
-        def _():
-            state_copy(j).wait_send()
 
 
 def per_device(
@@ -632,11 +636,12 @@
         name="layer",
         out_shape=pltpu.VMEM((TOK // 2, D), BF16),
         in_specs=[
-            pl.BlockSpec(memory_space=pltpu.SMEM), in_place, in_place, in_place, in_place,
+            in_place, in_place, in_place, in_place, in_place,
             in_place, in_place, in_place, in_place, in_place,
         ],
         out_specs=in_vmem,
         scratch_shapes=[
+            vmem((LOCAL, HEADS), F32),
             vmem((1, TOK), jnp.int32),
             vmem((LOCAL, HEADS, D), BF16),
             vmem((LOCAL, HEADS, D), BF16),
@@ -669,7 +674,7 @@
             vmem((TOK // 2, WIDTH), BF16),
             vmem((WIDTH, D), BF16),
             vmem((WIDTH, D), BF16),
-            dma((7,)), dma((2, LOCAL)), dma((LOCAL,)),
+            dma((8,)), dma((2, LOCAL)), dma((LOCAL,)),
             dma((MEM, LOCAL)), dma((MEM, LOCAL)), dma((MEM,)), dma((MEM,)),
             dma((MEM, LOCAL)), dma((MEM, LOCAL)),
             dma((CTX,)), dma((CTX,)), dma((CTX,)), dma((CTX,)),

time: 71.7 us -> 70.7 us (0.986)
  no operation moved by 1% of the time
where the time goes in v10:
time: 70.7 us; the launch traced here: 70.2 us
  Pallas kernels  69.2 us (98%)
  local copies, waits for them, and re-layouts  0.97 us (1%)
    pallas_call x1, Pallas kernels, per_device(): pl.pallas_call(layer_kernel, name='layer', out_shape=pltpu.VMEM((TOK // 2...  69.2 us

profile of v10, /device:TPU:25, one launch (start us, length us, event | category | flops | bytes accessed | tf_op | source)
XLA Modules:
  0.0 70.2 jit_solution(17547737711325700227)
XLA Ops:
  0.0 69.2 %layer.1 = bf16[256,2048]{1,0:T(8,128)(2,1)S(1)} custom-call(f32[4,4]{1,0:T(4,128)} %rate_hbm.1, s32[1,512]{1,0:T(1,128)} %bitcast.6, bf16[512,2048]{1,0:T(8,128)(2,1)} %tok_ref.1, bf16[2048,512]{1,0:T(8,128)(2,1)} %wq_ref.1, bf16[4,2048,512]{2,1,0:T(8,128)(2,1)} %wk_ref.1, bf16[4,2048,512]{2,1,0:T(8,128)(2,1)} %wv_ref.1, bf16[4,4,2048]{2,1,0:T(4,128)(2,1)} %bitcast.4, ...), custom_call_target="tpu_custom_call" | custom-call | tf_op jit(solution)/shard_map/layer/pallas_call | solution.py:634
  69.3 1.0 %copy.12 = bf16[256,2048]{1,0:T(8,128)(2,1)} copy(bf16[256,2048]{1,0:T(8,128)(2,1)S(1)} %layer.1) | data formatting | bytes 2097152

commit v11 on v10

--- a/solution.py
+++ b/solution.py
@@ -100,7 +100,7 @@
 def layer_kernel(
     rate_hbm, routes_hbm, tok_ref, wq_ref, wk_ref, wv_ref, wb_hbm, wd_hbm, gain_hbm, wo_ref,
     out_ref,
-    rate_ref, routes_ref, wb_ref, wd_ref, gain_ref, tok, outgoing, counts, cnt, xbuf, wq, wk, wv, gates, kv, logits_s, fades, total_ts, keys_s, solved_hi,
+    upper_s, select_s, rate_ref, routes_ref, wb_ref, wd_ref, gain_ref, tok, outgoing, counts, cnt, xbuf, wq, wk, wv, gates, kv, logits_s, fades, total_ts, keys_s, solved_hi,
     solved_lo, mw, maps, states, entering, base, reach, reply, returned, picked, partner, wo,
     w_other,
     load_sem, wkv_sem, own_sem, x_send, x_recv, c_send, c_recv, f_send, f_recv,
@@ -241,6 +241,11 @@
             x_arrival(d, m).wait_recv()
             forward(d, m).start()
 
+    gates[...] = jnp.zeros_like(gates)
+    upper_s[...] = ones_where(iota((ROWS, ROWS), 0) <= iota((ROWS, ROWS), 1))
+    at_gate = iota((48, 2 * WIDTH), 0) & 15
+    select_s[...] = ones_where(at_gate == iota((48, 2 * WIDTH), 1) // K)
+
     pass_on(0)
     for d in range(1, MEM):
         src = lax.rem(z + MEM - d, MEM)
@@ -256,7 +261,6 @@
             device_id={"ctx": owner(m, h)}, device_id_type=MESH,
         )
 
-    gates[...] = jnp.zeros_like(gates)
     for load in small_loads:
         load.wait()
     square = iota((K, K), 0), iota((K, K), 1)
@@ -280,10 +284,12 @@
             axis=0,
         )
 
-    def wait_tokens(m):
+    def wait_loads(m):
         for copy in weights(m):
             copy.wait()
         own_copy(m).wait()
+
+    def wait_tokens(m):
         for d in range(MEM):
             forward_arrival(d, m).wait_recv()
 
@@ -328,7 +334,7 @@
         strength = jax.nn.sigmoid(logits) * live
         soft = jnp.maximum(logits, 0.0) + jnp.log1p(jnp.exp(-jnp.abs(logits)))
         forget = -rate * soft * live
-        upper = ones_where(iota((ROWS, ROWS), 0) <= iota((ROWS, ROWS), 1))
+        upper = upper_s[...]
         hi, mid = split(forget)
         low = (forget - hi.astype(F32) - mid.astype(F32)).astype(BF16)
         total_t = mm(hi, upper) + mm(mid, upper) + mm(low, upper)
@@ -336,10 +342,9 @@
         total_ts[m] = both_t
         b_hi, b_mid = split(both_t)
         b_low = (both_t - b_hi.astype(F32) - b_mid.astype(F32)).astype(BF16)
-        at_gate = iota((48, 2 * WIDTH), 0) & 15
         wide = lax.dot_general(
             jnp.concatenate([b_hi, b_mid, b_low], axis=0),
-            ones_where(at_gate == iota((48, 2 * WIDTH), 1) // K),
+            select_s[...],
             (((0,), (0,)), ((), ())),
             preferred_element_type=F32,
         )
@@ -471,9 +476,14 @@
     def _():
         entering[...] = jnp.zeros_like(entering)
 
+    wait_loads(0)
     wait_tokens(0)
     for work in projections(0):
         work()
+
+    @pl.loop(1, LOCAL)
+    def _(m):
+        wait_loads(m)
 
     @pl.loop(0, LOCAL - 1)
     def _(m):
@@ -641,6 +651,8 @@
         ],
         out_specs=in_vmem,
         scratch_shapes=[
+            vmem((ROWS, ROWS), BF16),
+            vmem((48, 2 * WIDTH), BF16),
             vmem((LOCAL, HEADS), F32),
             vmem((1, TOK), jnp.int32),
             vmem((LOCAL, HEADS, D), BF16),

time: 70.7 us -> 70.7 us (level)
  no operation moved by 1% of the time
where the time goes in v11:
time: 70.7 us; the launch traced here: 70.2 us
  Pallas kernels  69.2 us (98%)
  local copies, waits for them, and re-layouts  0.97 us (1%)
    pallas_call x1, Pallas kernels, per_device(): pl.pallas_call(layer_kernel, name='layer', out_shape=pltpu.VMEM((TOK // 2...  69.2 us

profile of v11, /device:TPU:25, one launch (start us, length us, event | category | flops | bytes accessed | tf_op | source)
XLA Modules:
  0.0 70.2 jit_solution(666639329678436048)
XLA Ops:
  0.0 69.2 %layer.1 = bf16[256,2048]{1,0:T(8,128)(2,1)S(1)} custom-call(f32[4,4]{1,0:T(4,128)} %rate_hbm.1, s32[1,512]{1,0:T(1,128)} %bitcast.6, bf16[512,2048]{1,0:T(8,128)(2,1)} %tok_ref.1, bf16[2048,512]{1,0:T(8,128)(2,1)} %wq_ref.1, bf16[4,2048,512]{2,1,0:T(8,128)(2,1)} %wk_ref.1, bf16[4,2048,512]{2,1,0:T(8,128)(2,1)} %wv_ref.1, bf16[4,4,2048]{2,1,0:T(4,128)(2,1)} %bitcast.4, ...), custom_call_target="tpu_custom_call" | custom-call | tf_op jit(solution)/shard_map/layer/pallas_call | solution.py:644
  69.2 1.0 %copy.12 = bf16[256,2048]{1,0:T(8,128)(2,1)} copy(bf16[256,2048]{1,0:T(8,128)(2,1)S(1)} %layer.1) | data formatting | bytes 2097152
